TPU v7x, 768 devices: a whole 4x8x12 slice. The times are simulated.
768 devices in a mesh: curve: 96 (over z, y), slab: 8 (over x, core).
Axes of the slice: x: 4, y: 8, z: 12, core: 2. Of those that a mesh axis runs over, the one named last changes fastest.
Arguments:
- state: float32 [5, 125, 8, 12288], P(None, None, 'slab', 'curve'), as said below
- levels: int32 [8, 12288], P('slab', 'curve'), may hold values from 0 to 2
- neighbours: int32 [6, 8, 12288], P(None, 'slab', 'curve'), may hold values from 0 to 98303, as said below
- shifts: int32 [8, 96], P('slab', 'curve'), may hold values from -32 to 32
Outputs:
- moved: float32 [5, 125, 8, 12288], P(None, None, 'slab', 'curve')
- mortar: float32 [5, 25, 8, 12288], P(None, None, 'slab', 'curve')
Inputs may be any that keep to these rules, and one draw needn't show every extreme that they name: `neighbours`: faces 0 and 1 name an element of the row before and the row after (cyclically), faces 2 and 3 one of the same row; for faces 0 to 3 the named element sits in the same block of 128 positions; face 4 names one of the same row in the same block or the block before, face 5 in the same block or the block after (cyclically over blocks). `state`: density and pressure positive.
All inputs are finite; a program needn't handle non-finite values.
Results may differ from a plain program's by a relative error of at most 0.00021.
Values sent between devices are 32-bit elements; how exact they have to be, the bound alone decides.
No kernel may reach another device: no remote copies, remote signals or barrier semaphores. Data moves between devices by JAX's collectives and lax.ppermute only.
A program may use at most 32 MiB of HBM per device.

v0:
```python
import jax
import jax.numpy as jnp
import numpy as np
from jax import lax
from jax.sharding import PartitionSpec as P

NV = 5
ORDER = 5
NODES = 125
FACE = 25


GAMMA = 1.4
CFL = 0.05
END_WEIGHT = 0.1


def padded(cells, sides, width):
    for axis, dim in sides:
        count = lax.axis_size(axis)
        head = lax.slice_in_dim(cells, 0, width, axis=dim)
        tail = lax.slice_in_dim(cells, cells.shape[dim] - width, cells.shape[dim], axis=dim)
        cells = jnp.concatenate(
            [
                lax.ppermute(tail, axis, [(i, (i + 1) % count) for i in range(count)]),
                cells,
                lax.ppermute(head, axis, [((i + 1) % count, i) for i in range(count)]),
            ],
            axis=dim,
        )
    return cells


def derivative_matrix():
    points = np.array([-1.0, -np.sqrt(3.0 / 7.0), 0.0, np.sqrt(3.0 / 7.0), 1.0])
    bary = np.array(
        [1.0 / np.prod([points[j] - points[k] for k in range(5) if k != j]) for j in range(5)]
    )
    table = np.zeros((5, 5))
    for i in range(5):
        for j in range(5):
            if i != j:
                table[i, j] = bary[j] / bary[i] / (points[i] - points[j])
        table[i, i] = -np.sum(table[i])
    return jnp.asarray(table, jnp.float32)


def euler_flux(u, d):
    density = u[0]
    momentum = u[1:4]
    energy = u[4]
    velocity = momentum / density
    press = (GAMMA - 1.0) * (energy - 0.5 * jnp.sum(momentum * velocity, axis=0))
    along = velocity[d]
    parts = [momentum[d]]
    for a in range(3):
        term = momentum[a] * along
        if a == d:
            term = term + press
        parts.append(term)
    parts.append((energy + press) * along)
    return jnp.stack(parts)


def wave_speed(u):
    velocity = u[1:4] / u[0]
    press = (GAMMA - 1.0) * (u[4] - 0.5 * jnp.sum(u[1:4] * velocity, axis=0))
    return jnp.sqrt(jnp.sum(velocity * velocity, axis=0)) + jnp.sqrt(GAMMA * press / u[0])


def rusanov(lower, upper, d, lam):
    return 0.5 * (euler_flux(lower, d) + euler_flux(upper, d)) - 0.5 * lam * (upper - lower)


def own_faces(u5):
    return [u5[:, :, :, 0], u5[:, :, :, 4], u5[:, :, 0], u5[:, :, 4], u5[:, 0], u5[:, 4]]


def onehot(axis, index):
    shape = [1, 1, 1, 1, 1]
    shape[axis] = 5
    return (jnp.arange(5) == index).astype(jnp.float32).reshape(shape)


def residual(u5, outer, scale, lam):
    table = derivative_matrix()
    high = lax.Precision.HIGHEST
    div = jnp.einsum("ai,vkjie->vkjae", table, euler_flux(u5, 0), precision=high)
    div = div + jnp.einsum("aj,vkjie->vkaie", table, euler_flux(u5, 1), precision=high)
    div = div + jnp.einsum("ak,vkjie->vajie", table, euler_flux(u5, 2), precision=high)
    faces = own_faces(u5)
    correct = jnp.zeros_like(u5)
    for d in range(3):
        axis = 3 - d
        inner_low = faces[2 * d]
        inner_high = faces[2 * d + 1]
        lift_low = (
            rusanov(outer[2 * d], inner_low, d, lam) - euler_flux(inner_low, d)
        ) / END_WEIGHT
        lift_high = (
            rusanov(inner_high, outer[2 * d + 1], d, lam) - euler_flux(inner_high, d)
        ) / END_WEIGHT
        correct = correct + jnp.expand_dims(lift_low, axis) * onehot(axis, 0)
        correct = correct - jnp.expand_dims(lift_high, axis) * onehot(axis, 4)
    return scale * (correct - div)


def on_device(state, levels, neighbours, shifts):
    count = state.shape[-1]
    u5 = state.reshape(NV, ORDER, ORDER, ORDER, count)
    scale = jnp.exp2(levels.reshape(count).astype(jnp.float32))
    speed = wave_speed(u5)
    lam, top = lax.pmax((jnp.max(speed), jnp.max(speed * scale)), ("curve", "slab"))
    faces = own_faces(u5)
    slab_ext = padded(jnp.stack([faces[0], faces[1]]), (("slab", 0),), 1)
    curve_ext = padded(jnp.stack([faces[4], faces[5]]), (("curve", 0),), 1)
    below_x, above_x = (slab_ext[0], slab_ext[3])
    below_z, above_z = (curve_ext[0], curve_ext[3])
    local = neighbours.reshape(6, count)
    offset = local % count
    mine = lax.axis_index("curve")
    elsewhere = (local // count % lax.axis_size("curve") != mine).astype(jnp.int32) * count
    slot = offset + elsewhere
    outer = [
        jnp.take(below_x, offset[0], axis=-1),
        jnp.take(above_x, offset[1], axis=-1),
        jnp.take(faces[3], offset[2], axis=-1),
        jnp.take(faces[2], offset[3], axis=-1),
        jnp.take(jnp.concatenate([faces[5], below_z], axis=-1), slot[4], axis=-1),
        jnp.take(jnp.concatenate([faces[4], above_z], axis=-1), slot[5], axis=-1),
    ]
    new = u5 + CFL / top * residual(u5, outer, scale, lam)
    most = count // 4
    moved_by = shifts.reshape(())
    width = most + 1
    window = padded(new, (("curve", 4),), width)
    start = width + moved_by
    upper = window[:, 4]
    before = lax.dynamic_slice_in_dim(upper, start - 1, count, 3)
    moved_block = lax.dynamic_slice_in_dim(window, start, count, 4)
    mflux = rusanov(before, moved_block[:, 0], 2, lam)
    moved = moved_block.reshape(NV, NODES, 1, count)
    mortar = mflux.reshape(NV, FACE, 1, count)
    return (moved, mortar)


def solution(mesh):
    placed = (
        P(None, None, "slab", "curve"),
        P("slab", "curve"),
        P(None, "slab", "curve"),
        P("slab", "curve"),
    )
    return jax.shard_map(
        on_device,
        mesh=mesh,
        in_specs=placed,
        out_specs=(P(None, None, "slab", "curve"), P(None, None, "slab", "curve")),
        check_vma=False,
    )
```

profile of v0, /device:TPU:1, one launch (start us, length us, event | category | flops | bytes accessed | tf_op | source)
XLA Modules:
  0.0 228.4 jit_solution(11273204941517328326)
XLA Ops:
  0.7 1.8 reduce.4
  2.6 0.7 copy.383
  3.3 2.6 %collective-permute-start = (f32[1,5,5,5,128]{4,3,2,1,0:T(8,128)}, f32[1,5,5,5,128]{4,3,2,1,0:T(8,128)}, u32[]{:S(2)}, u32[]{:S(2)}) collective-permute-start(f32[1,5,5,5,128]{4,3,2,1,0:T(8,128)} %bitcast.655), channel_id=1, source_target_pairs={{0,1},{1,2},{2,3},{3,4},{4,5},{5,6},{6,7},{7,0},{8,9},{9,10},{10,1... | collective-permute-start | bytes 192008 | tf_op jit(solution)/shard_map/ppermute | solution.py:25
  6.5 7.9 %collective-permute-start.1 = (f32[1,5,5,5,128]{4,3,2,1,0:T(8,128)}, f32[1,5,5,5,128]{4,3,2,1,0:T(8,128)}, u32[]{:S(2)}, u32[]{:S(2)}) collective-permute-start(f32[1,5,5,5,128]{4,3,2,1,0:T(8,128)} %bitcast.654), channel_id=1, source_target_pairs={{1,0},{2,1},{3,2},{4,3},{5,4},{6,5},{7,6},{0,7},{9,8},{10,9},{11,1... | collective-permute-start | bytes 192008 | tf_op jit(solution)/shard_map/ppermute | solution.py:27
  14.4 0.8 slice_bitcast_fusion.4
  15.2 9.3 %collective-permute-start.3 = (f32[1,5,5,5,128]{4,3,2,1,0:T(8,128)}, f32[1,5,5,5,128]{4,3,2,1,0:T(8,128)}, u32[]{:S(2)}, u32[]{:S(2)}) collective-permute-start(f32[1,5,5,5,128]{4,3,2,1,0:T(8,128)} %get-tuple-element.92), channel_id=1, source_target_pairs={{8,0},{16,8},{24,16},{32,24},{40,32},{48,40},{56,48},{64,56},{72,6... | collective-permute-start | bytes 192008 | tf_op jit(solution)/shard_map/ppermute | solution.py:27
  24.5 1.9 collective-permute-start.2
  26.4 0.7 fusion.94
  27.2 0.7 fusion.95
  32.9 1.6 multiply_reduce_fusion
  37.3 0.9 copy.101
  38.2 2.4 %gather_fusion.3 = f32[128,5,5,5]{3,2,1,0:T(8,128)} fusion(f32[5,5,5,128]{2,1,3,0:T(8,128)S(1)} %copy.101, s32[1024]{0:T(1024)S(1)} %pad_clamp_fusion.2), kind=kCustom, calls=%fused_computation.4.clone | custom fusion | bytes 128512 | tf_op jit(solution)/shard_map/jit(_take)/gather | solution.py:128
  40.6 2.2 copy.102
  43.6 0.9 copy.88
  44.5 2.4 %gather_fusion.2 = f32[128,5,5,5]{3,2,1,0:T(8,128)} fusion(f32[5,5,5,128]{2,1,3,0:T(8,128)S(1)} %copy.88, s32[1024]{0:T(1024)S(1)} %pad_clamp_fusion.3), kind=kCustom, calls=%fused_computation.3.clone | custom fusion | bytes 128512 | tf_op jit(solution)/shard_map/jit(_take)/gather | solution.py:127
  46.9 2.3 %copy.89 = f32[128,5,5,5]{0,3,2,1:T(8,128)S(1)} copy(f32[128,5,5,5]{3,2,1,0:T(8,128)} %gather_fusion.2) | data formatting | bytes 128000 | tf_op jit(solution)/shard_map/jit(_take)/gather | solution.py:127
  50.0 0.9 fusion.28
  50.9 0.9 broadcast_divide_fusion
  52.3 1.4 fusion.6
  53.7 1.4 fusion.8
  56.1 108.3 %all-reduce = (f32[]{:T(128)}, f32[]{:T(128)}) all-reduce(f32[]{:T(128)} %get-tuple-element.12, f32[]{:T(128)} %get-tuple-element.11), channel_id=1, replica_groups=mesh['curve'=96,'slab'=8] {'curve','slab'}, use_global_device_ids=true, to_apply=%region_7.9 | all-reduce | flops 2 | bytes 16 | tf_op jit(solution)/shard_map/pmax | solution.py:113
  166.3 1.7 copy.72
  168.0 2.5 %gather_fusion = f32[128,5,5,5]{3,2,1,0:T(8,128)} fusion(f32[5,5,5,128]{2,1,3,0:T(8,128)S(1)} %copy.72, s32[1024]{0:T(1024)} %pad_clamp_fusion.5), kind=kCustom, calls=%fused_computation.clone | custom fusion | bytes 128512 | tf_op jit(solution)/shard_map/jit(_take)/gather | solution.py:125
  170.5 2.2 copy.73
  173.5 1.7 copy.85
  175.2 2.5 %gather_fusion.1 = f32[128,5,5,5]{3,2,1,0:T(8,128)} fusion(f32[5,5,5,128]{2,1,3,0:T(8,128)S(1)} %copy.85, s32[1024]{0:T(1024)} %pad_clamp_fusion.4), kind=kCustom, calls=%fused_computation.2.clone | custom fusion | bytes 128512 | tf_op jit(solution)/shard_map/jit(_take)/gather | solution.py:126
  177.7 2.2 copy.86
  179.9 0.7 select_bitcast_fusion.4
  181.4 1.0 pad_maximum_fusion.2
  182.4 3.1 %copy.109 = f32[5,5,5,256]{2,1,3,0:T(8,128)} copy(f32[5,5,5,256]{3,2,1,0:T(8,128)S(1)} %pad_maximum_fusion.2) | data formatting | bytes 256000 | tf_op jit(solution)/shard_map/concatenate | solution.py:130
  185.5 3.4 %gather_fusion.5 = f32[128,5,5,5]{3,2,1,0:T(8,128)S(1)} fusion(f32[5,5,5,256]{2,1,3,0:T(8,128)} %copy.109, s32[1024]{0:T(1024)S(1)} %pad_clamp_fusion), kind=kCustom, calls=%fused_computation.5.clone | custom fusion | bytes 128512 | tf_op jit(solution)/shard_map/jit(_take)/gather | solution.py:130
  188.9 1.2 copy.110
  190.1 0.9 select_bitcast_fusion
  191.8 1.0 pad_maximum_fusion.1
  192.7 3.1 %copy.104 = f32[5,5,5,256]{2,1,3,0:T(8,128)} copy(f32[5,5,5,256]{3,2,1,0:T(8,128)S(1)} %pad_maximum_fusion.1) | data formatting | bytes 256000 | tf_op jit(solution)/shard_map/concatenate | solution.py:129
  195.9 3.4 %gather_fusion.4 = f32[128,5,5,5]{3,2,1,0:T(8,128)S(1)} fusion(f32[5,5,5,256]{2,1,3,0:T(8,128)} %copy.104, s32[1024]{0:T(1024)S(1)} %pad_clamp_fusion.1), kind=kCustom, calls=%fused_computation.1.clone | custom fusion | bytes 128512 | tf_op jit(solution)/shard_map/jit(_take)/gather | solution.py:129
  199.3 1.2 copy.105
  200.5 1.0 select_bitcast_fusion.1
  201.6 1.0 fusion.20
  202.6 1.0 fusion.15
  203.7 1.4 subtract_multiply_fusion.3
  205.1 0.9 fusion.5
  206.2 1.9 collective-permute-start.4
  208.2 6.7 %collective-permute-start.5 = (f32[5,5,5,5,33]{4,3,2,1,0:T(8,128)S(1)}, f32[5,5,5,5,33]{4,3,2,1,0:T(8,128)S(1)}, u32[]{:S(2)}, u32[]{:S(2)}) collective-permute-start(f32[5,5,5,5,33]{4,3,2,1,0:T(8,128)S(1)} %get-tuple-element.55), channel_id=1, source_target_pairs={{8,0},{16,8},{24,16},{32,24},{40,32},{48,40},{56,48},{64,56},{72,6... | collective-permute-start | bytes 247508 | tf_op jit(solution)/shard_map/ppermute | solution.py:27
  215.5 8.5 %collective-permute-done.4 = f32[5,5,5,5,33]{4,3,2,1,0:T(8,128)S(1)} collective-permute-done((f32[5,5,5,5,33]{4,3,2,1,0:T(8,128)S(1)}, f32[5,5,5,5,33]{4,3,2,1,0:T(8,128)S(1)}, u32[]{:S(2)}, u32[]{:S(2)}) %collective-permute-start.4) | collective-permute-done | bytes 82532 | tf_op jit(solution)/shard_map/ppermute | solution.py:25
  224.0 0.9 collective-permute-done.5
  226.6 1.0 reshape.832
  227.7 0.7 multiply_subtract_fusion
  (233 shorter events, 15.6 us)
Async XLA Ops:
  0.6 27.2 %copy-start = (f32[5,125,1,128]{3,2,1,0:T(1,128)S(1)}, f32[5,125,1,128]{3,2,1,0:T(1,128)}, u32[]{:S(2)}) copy-start(f32[5,125,1,128]{3,2,1,0:T(1,128)} %param.9) | copy-start | bytes 960004
  0.6 27.9 %copy-start.46 = (s32[6,1,128]{2,1,0:T(1,128)S(1)}, s32[6,1,128]{2,1,0:T(1,128)}, u32[]{:S(2)}) copy-start(s32[6,1,128]{2,1,0:T(1,128)} %param.11) | copy-start | bytes 9220
  0.6 33.9 %copy-start.51 = (s32[1,128]{1,0:T(1,128)S(1)}, s32[1,128]{1,0:T(1,128)}, u32[]{:S(2)}) copy-start(s32[1,128]{1,0:T(1,128)} %param.10) | copy-start | bytes 1540
  2.6 24.5 %copy-start.8 = (f32[5,5,5,1,128]{4,3,2,1,0:T(1,128)}, f32[5,5,5,1,128]{4,3,2,1,0:T(1,128)S(1)}, u32[]{:S(2)}) copy-start(f32[5,5,5,1,128]{4,3,2,1,0:T(1,128)S(1)} %get-tuple-element.68) | copy-start | bytes 192004
  2.6 25.2 %copy-start.9 = (f32[5,5,5,1,128]{4,3,2,1,0:T(1,128)}, f32[5,5,5,1,128]{4,3,2,1,0:T(1,128)S(1)}, u32[]{:S(2)}) copy-start(f32[5,5,5,1,128]{4,3,2,1,0:T(1,128)S(1)} %get-tuple-element.69) | copy-start | bytes 192004
  3.3 163.0 %collective-permute-start = (f32[1,5,5,5,128]{4,3,2,1,0:T(8,128)}, f32[1,5,5,5,128]{4,3,2,1,0:T(8,128)}, u32[]{:S(2)}, u32[]{:S(2)}) collective-permute-start(f32[1,5,5,5,128]{4,3,2,1,0:T(8,128)} %bitcast.655), channel_id=1, source_target_pairs={{0,1},{1,2},{2,3},{3,4},{4,5},{5,6},{6,7},{7,0},{8,9},{9,10},{10,1... | collective-permute-start | bytes 192008 | tf_op jit(solution)/shard_map/ppermute | solution.py:25
  6.5 166.4 %collective-permute-start.1 = (f32[1,5,5,5,128]{4,3,2,1,0:T(8,128)}, f32[1,5,5,5,128]{4,3,2,1,0:T(8,128)}, u32[]{:S(2)}, u32[]{:S(2)}) collective-permute-start(f32[1,5,5,5,128]{4,3,2,1,0:T(8,128)} %bitcast.654), channel_id=1, source_target_pairs={{1,0},{2,1},{3,2},{4,3},{5,4},{6,5},{7,6},{0,7},{9,8},{10,9},{11,1... | collective-permute-start | bytes 192008 | tf_op jit(solution)/shard_map/ppermute | solution.py:27
  15.2 165.6 %collective-permute-start.3 = (f32[1,5,5,5,128]{4,3,2,1,0:T(8,128)}, f32[1,5,5,5,128]{4,3,2,1,0:T(8,128)}, u32[]{:S(2)}, u32[]{:S(2)}) collective-permute-start(f32[1,5,5,5,128]{4,3,2,1,0:T(8,128)} %get-tuple-element.92), channel_id=1, source_target_pairs={{8,0},{16,8},{24,16},{32,24},{40,32},{48,40},{56,48},{64,56},{72,6... | collective-permute-start | bytes 192008 | tf_op jit(solution)/shard_map/ppermute | solution.py:27
  24.5 166.6 %collective-permute-start.2 = (f32[1,5,5,5,128]{4,3,2,1,0:T(8,128)}, f32[1,5,5,5,128]{4,3,2,1,0:T(8,128)}, u32[]{:S(2)}, u32[]{:S(2)}) collective-permute-start(f32[1,5,5,5,128]{4,3,2,1,0:T(8,128)} %get-tuple-element.93), channel_id=1, source_target_pairs={{0,8},{8,16},{16,24},{24,32},{32,40},{40,48},{48,56},{56,64},{64,7... | collective-permute-start | bytes 192008 | tf_op jit(solution)/shard_map/ppermute | solution.py:25
  27.1 5.1 %copy-start.29 = (f32[1,5,5,1,128]{4,3,2,1,0:T(1,128)}, f32[1,5,5,1,128]{4,3,2,1,0:T(1,128)S(1)}, u32[]{:S(2)}) copy-start(f32[1,5,5,1,128]{4,3,2,1,0:T(1,128)S(1)} %get-tuple-element.62) | copy-start | bytes 38404
  27.2 5.1 %copy-start.31 = (f32[1,5,5,1,128]{4,3,2,1,0:T(1,128)}, f32[1,5,5,1,128]{4,3,2,1,0:T(1,128)S(1)}, u32[]{:S(2)}) copy-start(f32[1,5,5,1,128]{4,3,2,1,0:T(1,128)S(1)} %get-tuple-element.59) | copy-start | bytes 38404
  28.5 7.5 %copy-start.6 = (f32[1,125,1,128]{3,2,1,0:T(1,128)}, f32[1,125,1,128]{3,2,1,0:T(1,128)S(1)}, u32[]{:S(2)}) copy-start(f32[1,125,1,128]{3,2,1,0:T(1,128)S(1)} %get-tuple-element.111) | copy-start | bytes 192004
  32.9 5.3 %copy-start.50 = (s32[128]{0:T(128)S(1)}, s32[128]{0:T(128)}, u32[]{:S(2)}) copy-start(s32[128]{0:T(128)} %get-tuple-element.156) | copy-start | bytes 1540
  38.2 4.6 %copy-start.45 = (pred[128]{0:T(512)(128)(4,1)S(1)}, pred[128]{0:T(512)(128)(4,1)}, u32[]{:S(2)}) copy-start(pred[128]{0:T(512)(128)(4,1)} %get-tuple-element.155) | copy-start | bytes 388
  40.6 3.9 %copy-start.49 = (s32[128]{0:T(128)S(1)}, s32[128]{0:T(128)}, u32[]{:S(2)}) copy-start(s32[128]{0:T(128)} %get-tuple-element.154) | copy-start | bytes 1540
  43.6 5.5 %copy-start.44 = (pred[128]{0:T(512)(128)(4,1)S(1)}, pred[128]{0:T(512)(128)(4,1)}, u32[]{:S(2)}) copy-start(pred[128]{0:T(512)(128)(4,1)} %get-tuple-element.153) | copy-start | bytes 388
  46.9 3.1 %copy-start.3 = (f32[3,125,128]{2,1,0:T(8,128)S(1)}, f32[3,125,128]{2,1,0:T(8,128)}, u32[]{:S(2)}) copy-start(f32[3,125,128]{2,1,0:T(8,128)} %get-tuple-element.9) | copy-start | bytes 576004
  46.9 3.1 %copy-start.10 = (f32[125,128]{1,0:T(8,128)S(1)}, f32[125,128]{1,0:T(8,128)}, u32[]{:S(2)}) copy-start(f32[125,128]{1,0:T(8,128)} %get-tuple-element.8) | copy-start | bytes 192004
  46.9 3.2 %copy-start.11 = (f32[125,128]{1,0:T(8,128)S(1)}, f32[125,128]{1,0:T(8,128)}, u32[]{:S(2)}) copy-start(f32[125,128]{1,0:T(8,128)} %get-tuple-element.10) | copy-start | bytes 192004
  46.9 5.0 %copy-start.7 = (f32[1,125,1,128]{3,2,1,0:T(1,128)S(1)}, f32[1,125,1,128]{3,2,1,0:T(1,128)}, u32[]{:S(2)}) copy-start(f32[1,125,1,128]{3,2,1,0:T(1,128)} %get-tuple-element.109) | copy-start | bytes 192004
  50.0 2.3 %copy-start.39 = (f32[5,5,1,1,1]{1,0,4,3,2:T(8,128)S(1)}, f32[5,5,1,1,1]{1,0,4,3,2:T(8,128)}, u32[]{:S(2)}) copy-start(f32[5,5,1,1,1]{1,0,4,3,2:T(8,128)} %constant.116) | copy-start | bytes 304
  51.9 3.2 %copy-start.13 = (f32[3,5,5,1,128]{4,3,2,1,0:T(1,128)S(1)}, f32[3,5,5,1,128]{4,3,2,1,0:T(1,128)}, u32[]{:S(2)}) copy-start(f32[3,5,5,1,128]{4,3,2,1,0:T(1,128)} %get-tuple-element.67) | copy-start | bytes 115204
  51.9 3.2 %copy-start.34 = (f32[1,5,5,1,128]{4,2,3,1,0:T(8,128)S(1)}, f32[1,5,5,1,128]{4,2,3,1,0:T(8,128)}, u32[]{:S(2)}) copy-start(f32[1,5,5,1,128]{4,2,3,1,0:T(8,128)} %copy.384) | copy-start | bytes 38404
  51.9 3.2 %copy-start.16 = (f32[5,5,5,128]{3,2,1,0:T(8,128)S(1)}, f32[5,5,5,128]{3,2,1,0:T(8,128)}, u32[]{:S(2)}) copy-start(f32[5,5,5,128]{3,2,1,0:T(8,128)} %constant_dynamic-update-slice_fusion.14) | copy-start | bytes 192004
  51.9 3.2 %copy-start.27 = (f32[1,5,5,1,128]{4,3,2,1,0:T(1,128)S(1)}, f32[1,5,5,1,128]{4,3,2,1,0:T(1,128)}, u32[]{:S(2)}) copy-start(f32[1,5,5,1,128]{4,3,2,1,0:T(1,128)} %get-tuple-element.58) | copy-start | bytes 38404
  51.9 3.2 %copy-start.32 = (f32[1,5,5,1,128]{4,3,2,1,0:T(1,128)S(1)}, f32[1,5,5,1,128]{4,3,2,1,0:T(1,128)}, u32[]{:S(2)}) copy-start(f32[1,5,5,1,128]{4,3,2,1,0:T(1,128)} %copy-done.31) | copy-start | bytes 38404
  52.0 3.2 %copy-start.38 = (f32[1,5,5,1,128]{4,3,2,1,0:T(1,128)S(1)}, f32[1,5,5,1,128]{4,3,2,1,0:T(1,128)}, u32[]{:S(2)}) copy-start(f32[1,5,5,1,128]{4,3,2,1,0:T(1,128)} %get-tuple-element.57) | copy-start | bytes 38404
  52.0 3.2 %copy-start.37 = (f32[1,5,5,128]{3,0,2,1:T(1,128)S(1)}, f32[1,5,5,128]{3,0,2,1:T(1,128)}, u32[]{:S(2)}) copy-start(f32[1,5,5,128]{3,0,2,1:T(1,128)} %get-tuple-element.63) | copy-start | bytes 38404
  52.0 3.3 %copy-start.12 = (f32[3,5,5,1,128]{4,3,2,1,0:T(1,128)S(1)}, f32[3,5,5,1,128]{4,3,2,1,0:T(1,128)}, u32[]{:S(2)}) copy-start(f32[3,5,5,1,128]{4,3,2,1,0:T(1,128)} %get-tuple-element.66) | copy-start | bytes 115204
  52.0 3.3 %copy-start.33 = (f32[1,5,5,1,128]{4,2,3,1,0:T(8,128)S(1)}, f32[1,5,5,1,128]{4,2,3,1,0:T(8,128)}, u32[]{:S(2)}) copy-start(f32[1,5,5,1,128]{4,2,3,1,0:T(8,128)} %copy.385) | copy-start | bytes 38404
  52.0 3.3 %copy-start.14 = (f32[5,5,5,128]{3,2,1,0:T(8,128)S(1)}, f32[5,5,5,128]{3,2,1,0:T(8,128)}, u32[]{:S(2)}) copy-start(f32[5,5,5,128]{3,2,1,0:T(8,128)} %constant_dynamic-update-slice_fusion.9) | copy-start | bytes 192004
  52.0 3.3 %copy-start.28 = (f32[1,5,5,1,128]{4,3,2,1,0:T(1,128)S(1)}, f32[1,5,5,1,128]{4,3,2,1,0:T(1,128)}, u32[]{:S(2)}) copy-start(f32[1,5,5,1,128]{4,3,2,1,0:T(1,128)} %get-tuple-element.61) | copy-start | bytes 38404
  52.0 3.3 %copy-start.30 = (f32[1,5,5,1,128]{4,3,2,1,0:T(1,128)S(1)}, f32[1,5,5,1,128]{4,3,2,1,0:T(1,128)}, u32[]{:S(2)}) copy-start(f32[1,5,5,1,128]{4,3,2,1,0:T(1,128)} %copy-done.29) | copy-start | bytes 38404
  52.1 3.2 %copy-start.36 = (f32[1,5,5,1,128]{4,3,2,1,0:T(1,128)S(1)}, f32[1,5,5,1,128]{4,3,2,1,0:T(1,128)}, u32[]{:S(2)}) copy-start(f32[1,5,5,1,128]{4,3,2,1,0:T(1,128)} %get-tuple-element.60) | copy-start | bytes 38404
  52.1 3.3 %copy-start.35 = (f32[1,5,5,1,128]{4,3,2,1,0:T(1,128)S(1)}, f32[1,5,5,1,128]{4,3,2,1,0:T(1,128)}, u32[]{:S(2)}) copy-start(f32[1,5,5,1,128]{4,3,2,1,0:T(1,128)} %get-tuple-element.56) | copy-start | bytes 38404
  52.1 3.3 %copy-start.47 = (f32[128]{0:T(128)S(1)}, f32[128]{0:T(128)}, u32[]{:S(2)}) copy-start(f32[128]{0:T(128)} %exponential_bitcast_fusion) | copy-start | bytes 1540
  52.2 114.0 %copy-start.4 = (f32[5,5,5,5,128]{4,3,2,1,0:T(8,128)}, f32[5,5,5,5,128]{4,3,2,1,0:T(8,128)S(1)}, u32[]{:S(2)}) copy-start(f32[5,5,5,5,128]{4,3,2,1,0:T(8,128)S(1)} %get-tuple-element.99) | copy-start | bytes 960004
  55.4 110.9 %copy-start.15 = (f32[5,5,5,128]{3,2,1,0:T(8,128)}, f32[5,5,5,128]{3,2,1,0:T(8,128)S(1)}, u32[]{:S(2)}) copy-start(f32[5,5,5,128]{3,2,1,0:T(8,128)S(1)} %get-tuple-element.159) | copy-start | bytes 192004
  55.4 110.9 %copy-start.17 = (f32[5,5,5,128]{3,2,1,0:T(8,128)}, f32[5,5,5,128]{3,2,1,0:T(8,128)S(1)}, u32[]{:S(2)}) copy-start(f32[5,5,5,128]{3,2,1,0:T(8,128)S(1)} %get-tuple-element.160) | copy-start | bytes 192004
  166.3 6.4 %copy-start.42 = (pred[128]{0:T(512)(128)(4,1)S(1)}, pred[128]{0:T(512)(128)(4,1)}, u32[]{:S(2)}) copy-start(pred[128]{0:T(512)(128)(4,1)} %get-tuple-element.157) | copy-start | bytes 388
  199.2 5.8 %copy-start.40 = (f32[5]{0:T(128)S(1)}, f32[5]{0:T(128)}, u32[]{:S(2)}) copy-start(f32[5]{0:T(128)} %get-tuple-element.161) | copy-start | bytes 64
  199.2 5.8 %copy-start.41 = (f32[5]{0:T(128)S(1)}, f32[5]{0:T(128)}, u32[]{:S(2)}) copy-start(f32[5]{0:T(128)} %get-tuple-element.162) | copy-start | bytes 64
  200.5 4.6 %copy-start.1 = (f32[5,5,5,128,5]{3,4,2,1,0:T(8,128)S(1)}, f32[5,5,5,128,5]{3,4,2,1,0:T(8,128)}, u32[]{:S(2)}) copy-start(f32[5,5,5,128,5]{3,4,2,1,0:T(8,128)} %fusion.6) | copy-start | bytes 960004
  200.5 4.6 %copy-start.2 = (f32[5,5,5,128,5]{3,4,2,1,0:T(8,128)S(1)}, f32[5,5,5,128,5]{3,4,2,1,0:T(8,128)}, u32[]{:S(2)}) copy-start(f32[5,5,5,128,5]{3,4,2,1,0:T(8,128)} %fusion.8) | copy-start | bytes 960004
  200.5 4.6 %copy-start.5 = (f32[5,5,5,5,128]{4,3,2,1,0:T(8,128)S(1)}, f32[5,5,5,5,128]{4,3,2,1,0:T(8,128)}, u32[]{:S(2)}) copy-start(f32[5,5,5,5,128]{4,3,2,1,0:T(8,128)} %copy-done.4) | copy-start | bytes 960004
  200.5 4.6 %copy-start.48 = (f32[128]{0:T(128)S(1)}, f32[128]{0:T(128)}, u32[]{:S(2)}) copy-start(f32[128]{0:T(128)} %exponential_bitcast_fusion) | copy-start | bytes 1540
  206.2 17.8 %collective-permute-start.4 = (f32[5,5,5,5,33]{4,3,2,1,0:T(8,128)S(1)}, f32[5,5,5,5,33]{4,3,2,1,0:T(8,128)S(1)}, u32[]{:S(2)}, u32[]{:S(2)}) collective-permute-start(f32[5,5,5,5,33]{4,3,2,1,0:T(8,128)S(1)} %get-tuple-element.54), channel_id=1, source_target_pairs={{0,8},{8,16},{16,24},{24,32},{32,40},{40,48},{48,56},{56,64},{64,7... | collective-permute-start | bytes 247508 | tf_op jit(solution)/shard_map/ppermute | solution.py:25
  208.2 16.7 %collective-permute-start.5 = (f32[5,5,5,5,33]{4,3,2,1,0:T(8,128)S(1)}, f32[5,5,5,5,33]{4,3,2,1,0:T(8,128)S(1)}, u32[]{:S(2)}, u32[]{:S(2)}) collective-permute-start(f32[5,5,5,5,33]{4,3,2,1,0:T(8,128)S(1)} %get-tuple-element.55), channel_id=1, source_target_pairs={{8,0},{16,8},{24,16},{32,24},{40,32},{48,40},{56,48},{64,56},{72,6... | collective-permute-start | bytes 247508 | tf_op jit(solution)/shard_map/ppermute | solution.py:27
  (10 other events, 7.1 us)
where the time goes:
time: 230 us; the launch traced here: 228 us
  blocking collectives  108 us (47%)
  local copies, waits for them, and re-layouts  53.2 us (23%)
  starting transfers between devices  30.3 us (13%)
  other arithmetic  19.4 us (8%)
  waiting for transfers between devices  9.4 us (4%)
  between operations  4.01 us (2%)
  matrix products  3.75 us (2%)
    pmax x1, blocking collectives, on_device(): lax.pmax((jnp.max(speed), jnp.max(speed * scale)), ('curve', 'slab'))  108 us
    ppermute x3, starting transfers between devices, padded(): lax.ppermute(head, axis, [((i + 1) % count, i) for i in range(count)])  23.9 us
    ppermute x3, waiting for transfers between devices, padded(): lax.ppermute(tail, axis, [(i, (i + 1) % count) for i in range(count)])  8.49 us
    unnamed x121, local copies, waits for them, and re-layouts  8.45 us
    ppermute x3, starting transfers between devices, padded(): lax.ppermute(tail, axis, [(i, (i + 1) % count) for i in range(count)])  6.43 us
    gather x2, local copies, waits for them, and re-layouts, on_device(): jnp.take(above_x, offset[1], axis=-1)  4.72 us
    gather x2, local copies, waits for them, and re-layouts, on_device(): jnp.take(below_x, offset[0], axis=-1)  4.71 us
    gather x2, local copies, waits for them, and re-layouts, on_device(): jnp.take(faces[3], offset[2], axis=-1)  4.64 us
  transfers between devices with their start and end apart: 6, of which 2 were waited for; matrix products, arithmetic and copies ran while one was open for 23% of the time, Pallas kernels for 0%

commit v1 on v0

v1 whole, which is shorter than its diff:
```python
import jax
import jax.numpy as jnp
import numpy as np
from jax import lax
from jax.experimental import pallas as pl
from jax.experimental.pallas import tpu as pltpu
from jax.sharding import PartitionSpec as P

NV = 5
NODES = 125
FACE = 25
EL = 128
GAMMA = 1.4
CFL = 0.05
END_WEIGHT = 0.1
PAD = 128
FPAD = 32
LANES = 42
Z, Y, X, CORES = 12, 8, 4, 2
HIGH = lax.Precision.HIGHEST
AXES = ("curve", "slab")


def flat(z, y, x, core):
    return (z * Y + y) * X * CORES + x * CORES + core


def plane_groups():
    return [
        [flat(z, y, x, c) for y in range(Y) for x in range(X)] for z in range(Z) for c in range(CORES)
    ]


def column_groups():
    return [
        [flat(z, y, x, c) for z in range(Z) for c in range(CORES)] for y in range(Y) for x in range(X)
    ]


def derivative_matrix():
    points = np.array([-1.0, -np.sqrt(3.0 / 7.0), 0.0, np.sqrt(3.0 / 7.0), 1.0])
    bary = np.array(
        [1.0 / np.prod([points[j] - points[k] for k in range(5) if k != j]) for j in range(5)]
    )
    table = np.zeros((5, 5))
    for i in range(5):
        for j in range(5):
            if i != j:
                table[i, j] = bary[j] / bary[i] / (points[i] - points[j])
        table[i, i] = -np.sum(table[i])
    return table


def face_nodes(f):
    d, end = f // 2, 4 * (f % 2)
    nodes = []
    for b in range(5):
        for a in range(5):
            ijk = {0: (end, a, b), 1: (a, end, b), 2: (a, b, end)}[d]
            nodes.append(ijk[0] + 5 * ijk[1] + 25 * ijk[2])
    return nodes


def operator_table():
    half = 0.5 / END_WEIGHT
    table = derivative_matrix()
    eye = np.eye(5)
    volume = np.zeros((PAD, 3 * PAD))
    for d, parts in enumerate(((eye, eye, table), (eye, table, eye), (table, eye, eye))):
        full = np.kron(parts[0], np.kron(parts[1], parts[2]))
        volume[:NODES, d * PAD : d * PAD + NODES] = -full
    place = np.zeros((PAD, 6 * FPAD))
    count = np.zeros((PAD, 1))
    for f in range(6):
        sign = 1.0 - 2.0 * (f % 2)
        for m, n in enumerate(face_nodes(f)):
            place[n, f * FPAD + m] = 1.0
            volume[n, (f // 2) * PAD + n] -= sign * half
            count[n, 0] += half
    return np.concatenate([volume, place, np.broadcast_to(count, (PAD, EL))], axis=1).astype(np.float32)


def flux(u, d):
    density, momentum, energy = u[0], u[1:4], u[4]
    inverse = 1.0 / density
    velocity = [m * inverse for m in momentum]
    kinetic = momentum[0] * velocity[0] + momentum[1] * velocity[1] + momentum[2] * velocity[2]
    press = (GAMMA - 1.0) * (energy - 0.5 * kinetic)
    along = velocity[d]
    parts = [momentum[d]]
    for a in range(3):
        term = momentum[a] * along
        parts.append(term + press if a == d else term)
    parts.append((energy + press) * along)
    return parts


def all_fluxes(u):
    density, momentum, energy = u[0], u[1:4], u[4]
    inverse = 1.0 / density
    velocity = [m * inverse for m in momentum]
    kinetic = momentum[0] * velocity[0] + momentum[1] * velocity[1] + momentum[2] * velocity[2]
    press = (GAMMA - 1.0) * (energy - 0.5 * kinetic)
    total = energy + press
    out = []
    for d in range(3):
        along = velocity[d]
        parts = [momentum[d]]
        for a in range(3):
            term = momentum[a] * along
            parts.append(term + press if a == d else term)
        parts.append(total * along)
        out.append(parts)
    return out


def lane_pair(lam, top):
    lane = lax.broadcasted_iota(jnp.int32, (1, EL), 1)
    return jnp.where(lane < EL // 2, lam, top)


def start_kernel(state, levels, u, scale_row, peak, xlo, xhi, zlo, zhi, level, sem):
    copies = [
        pltpu.make_async_copy(state.at[v, :, 0], u.at[v, pl.ds(0, NODES)], sem.at[v]) for v in range(NV)
    ]
    copies.append(pltpu.make_async_copy(levels, level, sem.at[NV]))
    for copy in copies:
        copy.start()
    for v in range(NV):
        u[v, NODES:PAD, :] = jnp.full((PAD - NODES, EL), 1.0 if v == 0 else 0.0, jnp.float32)
    for copy in copies:
        copy.wait()
    scale = jnp.exp2(level[...].astype(jnp.float32))
    scale_row[...] = scale
    density, energy = u[0], u[4]
    momentum = [u[1], u[2], u[3]]
    inverse = 1.0 / density
    velocity = [m * inverse for m in momentum]
    kinetic = momentum[0] * velocity[0] + momentum[1] * velocity[1] + momentum[2] * velocity[2]
    press = (GAMMA - 1.0) * (energy - 0.5 * kinetic)
    square = velocity[0] * velocity[0] + velocity[1] * velocity[1] + velocity[2] * velocity[2]
    speed = jnp.sqrt(square) + jnp.sqrt(GAMMA * press * inverse)
    speed = jnp.max(speed, axis=0, keepdims=True)
    lam = jnp.max(speed, axis=1, keepdims=True)
    top = jnp.max(speed * scale, axis=1, keepdims=True)
    peak[...] = jnp.broadcast_to(lane_pair(lam, top)[None], peak.shape)
    ones = jnp.full((FPAD - FACE, EL), 1.0, jnp.float32)
    for v in range(NV):
        row = v * FPAD
        xlo[row : row + FACE, :] = u[v, pl.ds(0, FACE, stride=5), :]
        xhi[row : row + FACE, :] = u[v, pl.ds(4, FACE, stride=5), :]
        zlo[row : row + FACE, :] = u[v, 0:FACE, :]
        zhi[row : row + FACE, :] = u[v, NODES - FACE : NODES, :]
        for ref in (xlo, xhi, zlo, zhi):
            ref[row + FACE : row + FPAD, :] = ones


def dot(a, b):
    return jnp.dot(a, b, precision=HIGH, preferred_element_type=jnp.float32)


def middle_kernel(
    u, xlo, xhi, zlo, zhi, xbelow, xabove, zbelow, zabove, neighbours, scale_row, peaks, operator,
    a_out, b_out, to_left, to_right, peak, ylo, yhi, rhs, outer,
):
    best = jnp.max(peaks[...], axis=0)
    peak[...] = jnp.broadcast_to(best[None], peak.shape)
    scale = scale_row[...]
    ones = jnp.full((FPAD - FACE, EL), 1.0, jnp.float32)
    for v in range(NV):
        row = v * FPAD
        for k in range(5):
            ylo[row + 5 * k : row + 5 * k + 5, :] = u[v, 25 * k : 25 * k + 5, :]
            yhi[row + 5 * k : row + 5 * k + 5, :] = u[v, 25 * k + 20 : 25 * k + 25, :]
        ylo[row + FACE : row + FPAD, :] = ones
        yhi[row + FACE : row + FPAD, :] = ones
    for d, parts in enumerate(all_fluxes([u[v] for v in range(NV)])):
        for v in range(NV):
            rhs[d * PAD : (d + 1) * PAD, v * EL : (v + 1) * EL] = parts[v]
    source = lax.broadcasted_iota(jnp.int32, (EL, EL), 0)
    named = [neighbours[f] for f in range(6)]
    home = named[2] >> 7
    half = 0.5 / END_WEIGHT
    for f in range(6):
        offset = named[f] & (EL - 1)
        if f < 4:
            trace = (xbelow, xabove, yhi, ylo)[f]
            got = dot(trace[...], (source == offset).astype(jnp.float32))
        else:
            here = (named[f] >> 7) == home
            mine, other = ((zhi, zbelow), (zlo, zabove))[f - 4]
            own_index = jnp.where(here, offset, -1)
            other_index = jnp.where(here, -1, offset)
            got = dot(mine[...], (source == own_index).astype(jnp.float32)) + dot(
                other[...], (source == other_index).astype(jnp.float32)
            )
        got = [got[v * FPAD : (v + 1) * FPAD] for v in range(NV)]
        sign = half * (1.0 - 2.0 * (f % 2))
        parts = flux(got, f // 2)
        for v in range(NV):
            rhs[3 * PAD + f * FPAD : 3 * PAD + (f + 1) * FPAD, v * EL : (v + 1) * EL] = sign * parts[v]
            outer[f * FPAD : (f + 1) * FPAD, v * EL : (v + 1) * EL] = half * got[v]
    place = 3 * PAD + 6 * FPAD
    a = dot(operator[:, :place], rhs[...])
    b = dot(operator[:, 3 * PAD : place], outer[...])
    count = operator[:, place:]
    lane = lax.broadcasted_iota(jnp.int32, (PAD, EL), 1)
    for v in range(NV):
        uv = u[v]
        av = a[:, v * EL : (v + 1) * EL] * scale
        bv = (b[:, v * EL : (v + 1) * EL] - count * uv) * scale
        a_out[v] = av
        b_out[v] = bv
        to_left[v] = jnp.where(
            lane < LANES,
            uv,
            jnp.where(lane < 2 * LANES, pltpu.roll(av, LANES, 1), pltpu.roll(bv, 2 * LANES, 1)),
        )
        to_right[v] = jnp.where(
            lane < LANES,
            pltpu.roll(uv, LANES, 1),
            jnp.where(lane < 2 * LANES, pltpu.roll(av, 2 * LANES, 1), pltpu.roll(bv, 3 * LANES, 1)),
        )


def last_kernel(shifts, u, a, b, from_left, from_right, peaks, moved, mortar, new, surface, sem):
    best = jnp.max(peaks[...], axis=0)
    lam = jnp.max(best[:, : EL // 2], axis=1, keepdims=True)
    top = jnp.max(best[:, EL // 2 :], axis=1, keepdims=True)
    step = CFL / top
    shift = shifts[0, 0]
    ahead = shift >= 1
    turn = jnp.where(ahead, 2 * EL - shift, 2 * EL - shift - LANES) % EL
    own_turn = (2 * EL - shift) % EL
    lane = lax.broadcasted_iota(jnp.int32, (PAD, EL), 1)
    first = jnp.where(ahead, EL - shift, 0)
    end = jnp.where(ahead, EL, -shift)
    outside = (lane >= first) & (lane < end)
    lane_up = lax.broadcasted_iota(jnp.int32, (FPAD, EL), 1)
    outside_up = (lane_up >= jnp.where(ahead, first + 1, 0)) & (lane_up < end + 1)
    low, high = [], []
    copies = []
    for v in range(NV):
        own = u[v] + step * (a[v] + lam * b[v])
        pack = jnp.where(ahead, from_right[v], from_left[v])
        halo = pack + step * (pltpu.roll(pack, EL - LANES, 1) + lam * pltpu.roll(pack, EL - 2 * LANES, 1))
        own = pltpu.roll(own, own_turn, 1)
        halo = pltpu.roll(halo, turn, 1)
        block = jnp.where(outside, halo, own)
        new[v] = block
        copy = pltpu.make_async_copy(new.at[v, pl.ds(0, NODES)], moved.at[v, :, 0], sem.at[v])
        copy.start()
        copies.append(copy)
        low.append(block[:FPAD])
        before = jnp.where(
            outside_up, pltpu.roll(halo[PAD - FPAD :], 1, 1), pltpu.roll(own[PAD - FPAD :], 1, 1)
        )
        high.append(pltpu.roll(before, FPAD - 4, 0))
    lower, upper = flux(high, 2), flux(low, 2)
    for v in range(NV):
        surface[v] = 0.5 * (lower[v] + upper[v]) - 0.5 * lam * (low[v] - high[v])
        copy = pltpu.make_async_copy(
            surface.at[v, pl.ds(0, FACE)], mortar.at[v, :, 0], sem.at[NV + v]
        )
        copy.start()
        copies.append(copy)
    for copy in copies:
        copy.wait()


def shape(*dims):
    return jax.ShapeDtypeStruct(dims, jnp.float32)


VMEM = pl.BlockSpec(memory_space=pltpu.VMEM)
ANY = pl.BlockSpec(memory_space=pl.ANY)
HBM = pl.BlockSpec(memory_space=pltpu.HBM)
SMEM = pl.BlockSpec(memory_space=pltpu.SMEM)


def shifted(value, axis, step):
    count = lax.axis_size(axis)
    return lax.ppermute(value, axis, [(i, (i + step) % count) for i in range(count)])


def exchanged(value, groups):
    return lax.all_to_all(value, AXES, 0, 0, tiled=True, axis_index_groups=groups)


def on_device(state, levels, neighbours, shifts):
    planes, columns = plane_groups(), column_groups()
    operator = jnp.asarray(operator_table())
    trace = shape(NV * FPAD, EL)
    block = shape(NV, PAD, EL)
    u, scale, peak, xlo, xhi, zlo, zhi = pl.pallas_call(
        start_kernel,
        out_shape=(block, shape(1, EL), shape(len(planes[0]), 1, EL), trace, trace, trace, trace),
        in_specs=[HBM, HBM],
        out_specs=(VMEM,) * 7,
        scratch_shapes=[pltpu.VMEM((1, EL), jnp.int32), pltpu.SemaphoreType.DMA((NV + 1,))],
        compiler_params=pltpu.CompilerParams(vmem_limit_bytes=4 << 20),
        name="start",
    )(pltpu.with_memory_space_constraint(state, pltpu.HBM), pltpu.with_memory_space_constraint(levels, pltpu.HBM))
    xbelow = shifted(xhi, "slab", 1)
    xabove = shifted(xlo, "slab", -1)
    zbelow = shifted(zhi, "curve", 1)
    zabove = shifted(zlo, "curve", -1)
    peak = exchanged(peak, planes)
    a, b, to_left, to_right, peak = pl.pallas_call(
        middle_kernel,
        out_shape=(block, block, block, block, shape(len(columns[0]), 1, EL)),
        in_specs=[VMEM] * 13,
        out_specs=(VMEM,) * 5,
        scratch_shapes=[
            pltpu.VMEM((NV * FPAD, EL), jnp.float32),
            pltpu.VMEM((NV * FPAD, EL), jnp.float32),
            pltpu.VMEM((3 * PAD + 6 * FPAD, NV * EL), jnp.float32),
            pltpu.VMEM((6 * FPAD, NV * EL), jnp.float32),
        ],
        compiler_params=pltpu.CompilerParams(vmem_limit_bytes=12 << 20),
        name="middle",
    )(
        u, xlo, xhi, zlo, zhi, xbelow, xabove, zbelow, zabove, neighbours, scale, peak, operator
    )
    from_left = shifted(to_right, "curve", 1)
    from_right = shifted(to_left, "curve", -1)
    peak = exchanged(peak, columns)
    return pl.pallas_call(
        last_kernel,
        out_shape=(shape(NV, NODES, 1, EL), shape(NV, FACE, 1, EL)),
        in_specs=[SMEM] + [VMEM] * 6,
        out_specs=(ANY, ANY),
        scratch_shapes=[
            pltpu.VMEM((NV, PAD, EL), jnp.float32),
            pltpu.VMEM((NV, FPAD, EL), jnp.float32),
            pltpu.SemaphoreType.DMA((2 * NV,)),
        ],
        compiler_params=pltpu.CompilerParams(vmem_limit_bytes=8 << 20),
        name="last",
    )(shifts, u, a, b, from_left, from_right, peak)


def solution(mesh):
    placed = (
        P(None, None, "slab", "curve"),
        P("slab", "curve"),
        P(None, "slab", "curve"),
        P("slab", "curve"),
    )
    return jax.shard_map(
        on_device,
        mesh=mesh,
        in_specs=placed,
        out_specs=(P(None, None, "slab", "curve"), P(None, None, "slab", "curve")),
        check_vma=False,
    )
```

time: 230 us -> 70.7 us (0.31)
  blocking collectives: 108 us -> 12.5 us
  local copies, waits for them, and re-layouts: 53.2 us -> 1.65 us
  other arithmetic: 19.4 us -> 0 us
  starting transfers between devices: 30.3 us -> 40.4 us
  Pallas kernels: 0 us -> 5.62 us
  matrix products: 3.75 us -> 0 us
  between operations: 4.01 us -> 1.35 us
    pmax x1 -> x0, blocking collectives: 108 us -> none  [on_device(): lax.pmax((jnp.max(speed), jnp.max(speed * scale)), ('curve', 'slab'))]
    gather x12 -> x0, local copies, waits for them, and re-layouts: 27.8 us -> none  [the longest x2 4.72 us: on_device(): jnp.take(above_x, offset[1], axis=-1)]
    all_to_all x0 -> x1, blocking collectives: none -> 12.5 us  [exchanged(): lax.all_to_all(value, AXES, 0, 0, tiled=True, axis_index_groups=groups)]
    all_to_all x0 -> x1, starting transfers between devices: none -> 9.81 us  [exchanged(): lax.all_to_all(value, AXES, 0, 0, tiled=True, axis_index_groups=groups)]
    ppermute x6, waiting for transfers between devices: 9.4 us -> 0.02 us  [shifted(): lax.ppermute(value, axis, [(i, (i + step) % count) for i in range(count)])]
    all_to_all x0 -> x1, waiting for transfers between devices: none -> 8.72 us  [exchanged(): lax.all_to_all(value, AXES, 0, 0, tiled=True, axis_index_groups=groups)]
    unnamed x121 -> x4, local copies, waits for them, and re-layouts: 8.45 us -> 1.65 us
    concatenate x2 -> x0, local copies, waits for them, and re-layouts: 6.27 us -> none  [the longest x1 3.14 us: on_device(): jnp.concatenate([faces[4], above_z], axis=-1)]
  transfers between devices with their start and end apart: 6 -> 7, of which waited for: 2 -> 1; matrix products, arithmetic and copies ran while one was open for 23% -> 0% of each run, Pallas kernels for 0% -> 0%
where the time goes in v1:
time: 70.7 us; the launch traced here: 70.3 us
  starting transfers between devices  40.4 us (57%)
  blocking collectives  12.5 us (18%)
  waiting for transfers between devices  8.74 us (12%)
  Pallas kernels  5.62 us (8%)
  local copies, waits for them, and re-layouts  1.65 us (2%)
  between operations  1.35 us (2%)
    ppermute x6, starting transfers between devices, shifted(): lax.ppermute(value, axis, [(i, (i + step) % count) for i in range(count)])  30.6 us
    all_to_all x1, blocking collectives, exchanged(): lax.all_to_all(value, AXES, 0, 0, tiled=True, axis_index_groups=groups)  12.5 us
    all_to_all x1, starting transfers between devices, exchanged(): lax.all_to_all(value, AXES, 0, 0, tiled=True, axis_index_groups=groups)  9.81 us
    all_to_all x1, waiting for transfers between devices, exchanged(): lax.all_to_all(value, AXES, 0, 0, tiled=True, axis_index_groups=groups)  8.72 us
    pallas_call x1, Pallas kernels, on_device(): pl.pallas_call(middle_kernel, out_shape=(block, block, block, block, shap...  2.93 us
    unnamed x4, local copies, waits for them, and re-layouts  1.65 us
    pallas_call x1, Pallas kernels, on_device(): pl.pallas_call(last_kernel, out_shape=(shape(NV, NODES, 1, EL), shape(NV,...  1.49 us
  transfers between devices with their start and end apart: 7, of which 1 were waited for; matrix products, arithmetic and copies ran while one was open for 0% of the time, Pallas kernels for 0%

profile of v1, /device:TPU:1, one launch (start us, length us, event | category | flops | bytes accessed | tf_op | source)
XLA Modules:
  0.0 70.3 jit_solution(15607855689032441835)
XLA Ops:
  0.6 1.2 %start.1 = (f32[5,128,128]{2,1,0:T(8,128)S(1)}, f32[1,128]{1,0:T(1,128)S(1)}, f32[32,1,128]{2,1,0:T(1,128)S(1)}, f32[160,128]{1,0:T(8,128)S(1)}, f32[160,128]{1,...) custom-call(f32[5,125,1,128]{3,2,1,0:T(1,128)} %state.1, s32[1,128]{1,0:T(1,128)} %levels.1), custom_call_target="tpu_custom_call" | custom-call | tf_op jit(solution)/shard_map/start/pallas_call | solution.py:295
  1.8 2.6 %collective-permute-start = (f32[160,128]{1,0:T(8,128)S(1)}, f32[160,128]{1,0:T(8,128)S(1)}, u32[]{:S(2)}, u32[]{:S(2)}) collective-permute-start(f32[160,128]{1,0:T(8,128)S(1)} %get-tuple-element.16.xhi), channel_id=1, source_target_pairs={{0,1},{1,2},{2,3},{3,4},{4,5},{5,6},{6,7},{7,0},{8,9},{9,10},{10,1... | collective-permute-start | bytes 245768 | tf_op jit(solution)/shard_map/ppermute | solution.py:283
  4.4 7.9 %collective-permute-start.1 = (f32[160,128]{1,0:T(8,128)S(1)}, f32[160,128]{1,0:T(8,128)S(1)}, u32[]{:S(2)}, u32[]{:S(2)}) collective-permute-start(f32[160,128]{1,0:T(8,128)S(1)} %get-tuple-element.15.xlo), channel_id=1, source_target_pairs={{0,7},{1,0},{2,1},{3,2},{4,3},{5,4},{6,5},{7,6},{8,15},{9,8},{10,9... | collective-permute-start | bytes 245768 | tf_op jit(solution)/shard_map/ppermute | solution.py:283
  12.4 1.9 %collective-permute-start.2 = (f32[160,128]{1,0:T(8,128)S(1)}, f32[160,128]{1,0:T(8,128)S(1)}, u32[]{:S(2)}, u32[]{:S(2)}) collective-permute-start(f32[160,128]{1,0:T(8,128)S(1)} %get-tuple-element.18.zhi), channel_id=1, source_target_pairs={{0,8},{8,16},{16,24},{24,32},{32,40},{40,48},{48,56},{56,64},{64,7... | collective-permute-start | bytes 245768 | tf_op jit(solution)/shard_map/ppermute | solution.py:283
  14.3 9.3 %collective-permute-start.3 = (f32[160,128]{1,0:T(8,128)S(1)}, f32[160,128]{1,0:T(8,128)S(1)}, u32[]{:S(2)}, u32[]{:S(2)}) collective-permute-start(f32[160,128]{1,0:T(8,128)S(1)} %get-tuple-element.17.zlo), channel_id=1, source_target_pairs={{0,760},{8,0},{16,8},{24,16},{32,24},{40,32},{48,40},{56,48},{64,5... | collective-permute-start | bytes 245768 | tf_op jit(solution)/shard_map/ppermute | solution.py:283
  23.6 12.5 %all_to_all.10.peaks = f32[32,1,128]{2,1,0:T(1,128)S(1)} all-to-all(f32[32,1,128]{2,1,0:T(1,128)S(1)} %get-tuple-element.20), channel_id=1, replica_groups={{0,2,4,6,8,10,12,14,16,18,20,22,24,26,28,30,32,34,36,38,40,42,44,46,48,..., dimensions={0} | all-to-all | bytes 32768 | tf_op jit(solution)/shard_map/all_to_all | solution.py:287
  36.1 0.0 copy-start.1
  36.1 0.0 collective-permute-done.xbelow
  36.1 0.0 collective-permute-done.1.xabove
  36.1 0.0 collective-permute-done.2.zbelow
  36.1 0.0 collective-permute-done.3.zabove
  36.1 0.7 copy-done.1
  36.8 0.0 copy-start
  36.8 1.0 %copy-done = f32[128,704]{1,0:T(8,128)S(1)} copy-done((f32[128,704]{1,0:T(8,128)S(1)}, f32[128,704]{1,0:T(8,128)}, u32[]{:S(2)}) %copy-start) | copy-done | bytes 360472
  37.8 2.9 %middle.1 = (f32[5,128,128]{2,1,0:T(8,128)S(1)}, f32[5,128,128]{2,1,0:T(8,128)S(1)}, f32[5,128,128]{2,1,0:T(8,128)S(1)}, f32[5,128,128]{2,1,0:T(8,128)S(1)}, f32[24,1,128]{2,1,0:T(1,128)}) custom-call(f32[5,128,128]{2,1,0:T(8,128)S(1)} %get-tuple-element.14.u, f32[160,128]{1,0:T(8,128)S(1)} %get-tuple-element.15.xlo, f32[160,128]{1,0:T(8,128)S(1)} %get-tuple-element.16.xhi, ...), custom_call_target="tpu_custom_call" | custom-call | tf_op jit(solution)/shard_map/middle/pallas_call | solution.py:309
  40.7 2.2 %collective-permute-start.4 = (f32[5,128,128]{2,1,0:T(8,128)S(1)}, f32[5,128,128]{2,1,0:T(8,128)S(1)}, u32[]{:S(2)}, u32[]{:S(2)}) collective-permute-start(f32[5,128,128]{2,1,0:T(8,128)S(1)} %get-tuple-element.23), channel_id=1, source_target_pairs={{0,8},{8,16},{16,24},{24,32},{32,40},{40,48},{48,56},{56,64},{64,7... | collective-permute-start | bytes 983048 | tf_op jit(solution)/shard_map/ppermute | solution.py:283
  43.0 6.7 %collective-permute-start.5 = (f32[5,128,128]{2,1,0:T(8,128)S(1)}, f32[5,128,128]{2,1,0:T(8,128)S(1)}, u32[]{:S(2)}, u32[]{:S(2)}) collective-permute-start(f32[5,128,128]{2,1,0:T(8,128)S(1)} %get-tuple-element.24), channel_id=1, source_target_pairs={{0,760},{8,0},{16,8},{24,16},{32,24},{40,32},{48,40},{56,48},{64,5... | collective-permute-start | bytes 983048 | tf_op jit(solution)/shard_map/ppermute | solution.py:283
  49.6 9.8 %all-to-all-start.1 = ((f32[24,1,128]{2,1,0:T(1,128)}), f32[24,1,128]{2,1,0:T(1,128)S(1)}, u32[]{:S(2)}, u32[]{:S(2)}) async-start(f32[24,1,128]{2,1,0:T(1,128)} %get-tuple-element.25), calls=%async_computation.1 | async-start | bytes 24576 | tf_op jit(solution)/shard_map/all_to_all | solution.py:287
  60.1 8.7 %all-to-all-done.1.peaks = f32[24,1,128]{2,1,0:T(1,128)S(1)} async-done(((f32[24,1,128]{2,1,0:T(1,128)}), f32[24,1,128]{2,1,0:T(1,128)S(1)}, u32[]{:S(2)}, u32[]{:S(2)}) %all-to-all-start.1) | async-done | bytes 12320 | tf_op jit(solution)/shard_map/all_to_all | solution.py:287
  68.8 0.0 collective-permute-done.4.from_left
  68.8 0.0 collective-permute-done.5.from_right
  68.8 1.5 %last.1 = (f32[5,125,1,128]{3,2,1,0:T(1,128)}, f32[5,25,1,128]{3,2,1,0:T(1,128)}) custom-call(s32[1,1]{1,0:T(1,128)S(6)} %copy.7.shifts, f32[5,128,128]{2,1,0:T(8,128)S(1)} %get-tuple-element.14.u, f32[5,128,128]{2,1,0:T(8,128)S(1)} %get-tuple-element.21.a, f32[5,128,128]{2,1,0:T(8,128)S(1)} %get-tuple-element.22.b, ...), custom_call_target="tpu_custom_call" | custom-call | tf_op jit(solution)/shard_map/last/pallas_call | solution.py:328
Async XLA Ops:
  1.8 34.3 %collective-permute-start = (f32[160,128]{1,0:T(8,128)S(1)}, f32[160,128]{1,0:T(8,128)S(1)}, u32[]{:S(2)}, u32[]{:S(2)}) collective-permute-start(f32[160,128]{1,0:T(8,128)S(1)} %get-tuple-element.16.xhi), channel_id=1, source_target_pairs={{0,1},{1,2},{2,3},{3,4},{4,5},{5,6},{6,7},{7,0},{8,9},{9,10},{10,1... | collective-permute-start | bytes 245768 | tf_op jit(solution)/shard_map/ppermute | solution.py:283
  4.4 31.7 %collective-permute-start.1 = (f32[160,128]{1,0:T(8,128)S(1)}, f32[160,128]{1,0:T(8,128)S(1)}, u32[]{:S(2)}, u32[]{:S(2)}) collective-permute-start(f32[160,128]{1,0:T(8,128)S(1)} %get-tuple-element.15.xlo), channel_id=1, source_target_pairs={{0,7},{1,0},{2,1},{3,2},{4,3},{5,4},{6,5},{7,6},{8,15},{9,8},{10,9... | collective-permute-start | bytes 245768 | tf_op jit(solution)/shard_map/ppermute | solution.py:283
  12.4 23.8 %collective-permute-start.2 = (f32[160,128]{1,0:T(8,128)S(1)}, f32[160,128]{1,0:T(8,128)S(1)}, u32[]{:S(2)}, u32[]{:S(2)}) collective-permute-start(f32[160,128]{1,0:T(8,128)S(1)} %get-tuple-element.18.zhi), channel_id=1, source_target_pairs={{0,8},{8,16},{16,24},{24,32},{32,40},{40,48},{48,56},{56,64},{64,7... | collective-permute-start | bytes 245768 | tf_op jit(solution)/shard_map/ppermute | solution.py:283
  14.3 21.9 %collective-permute-start.3 = (f32[160,128]{1,0:T(8,128)S(1)}, f32[160,128]{1,0:T(8,128)S(1)}, u32[]{:S(2)}, u32[]{:S(2)}) collective-permute-start(f32[160,128]{1,0:T(8,128)S(1)} %get-tuple-element.17.zlo), channel_id=1, source_target_pairs={{0,760},{8,0},{16,8},{24,16},{32,24},{40,32},{48,40},{56,48},{64,5... | collective-permute-start | bytes 245768 | tf_op jit(solution)/shard_map/ppermute | solution.py:283
  36.1 0.7 copy-start.1
  36.8 1.0 %copy-start = (f32[128,704]{1,0:T(8,128)S(1)}, f32[128,704]{1,0:T(8,128)}, u32[]{:S(2)}) copy-start(f32[128,704]{1,0:T(8,128)} %constant.2.clone.operator) | copy-start | bytes 1081348
  40.7 28.1 %collective-permute-start.4 = (f32[5,128,128]{2,1,0:T(8,128)S(1)}, f32[5,128,128]{2,1,0:T(8,128)S(1)}, u32[]{:S(2)}, u32[]{:S(2)}) collective-permute-start(f32[5,128,128]{2,1,0:T(8,128)S(1)} %get-tuple-element.23), channel_id=1, source_target_pairs={{0,8},{8,16},{16,24},{24,32},{32,40},{40,48},{48,56},{56,64},{64,7... | collective-permute-start | bytes 983048 | tf_op jit(solution)/shard_map/ppermute | solution.py:283
  43.0 25.9 %collective-permute-start.5 = (f32[5,128,128]{2,1,0:T(8,128)S(1)}, f32[5,128,128]{2,1,0:T(8,128)S(1)}, u32[]{:S(2)}, u32[]{:S(2)}) collective-permute-start(f32[5,128,128]{2,1,0:T(8,128)S(1)} %get-tuple-element.24), channel_id=1, source_target_pairs={{0,760},{8,0},{16,8},{24,16},{32,24},{40,32},{48,40},{56,48},{64,5... | collective-permute-start | bytes 983048 | tf_op jit(solution)/shard_map/ppermute | solution.py:283
  49.6 19.2 %all-to-all-start.1 = ((f32[24,1,128]{2,1,0:T(1,128)}), f32[24,1,128]{2,1,0:T(1,128)S(1)}, u32[]{:S(2)}, u32[]{:S(2)}) async-start(f32[24,1,128]{2,1,0:T(1,128)} %get-tuple-element.25), calls=%async_computation.1 | async-start | bytes 24576 | tf_op jit(solution)/shard_map/all_to_all | solution.py:287

commit v2 on v1

--- a/solution.py
+++ b/solution.py
@@ -5,6 +5,7 @@
 from jax.experimental import pallas as pl
 from jax.experimental.pallas import tpu as pltpu
 from jax.sharding import PartitionSpec as P
+
 
 NV = 5
 NODES = 125
@@ -161,8 +162,14 @@
 
 def middle_kernel(
     u, xlo, xhi, zlo, zhi, xbelow, xabove, zbelow, zabove, neighbours, scale_row, peaks, operator,
-    a_out, b_out, to_left, to_right, peak, ylo, yhi, rhs, outer,
+    a_out, b_out, to_left, to_right, peak, ylo, yhi, rhs, outer, named, table, sem,
 ):
+    fetches = [
+        pltpu.make_async_copy(neighbours, named, sem.at[0]),
+        pltpu.make_async_copy(operator, table, sem.at[1]),
+    ]
+    for fetch in fetches:
+        fetch.start()
     best = jnp.max(peaks[...], axis=0)
     peak[...] = jnp.broadcast_to(best[None], peak.shape)
     scale = scale_row[...]
@@ -178,7 +185,7 @@
         for v in range(NV):
             rhs[d * PAD : (d + 1) * PAD, v * EL : (v + 1) * EL] = parts[v]
     source = lax.broadcasted_iota(jnp.int32, (EL, EL), 0)
-    named = [neighbours[f] for f in range(6)]
+    fetches[0].wait()
     home = named[2] >> 7
     half = 0.5 / END_WEIGHT
     for f in range(6):
@@ -201,9 +208,10 @@
             rhs[3 * PAD + f * FPAD : 3 * PAD + (f + 1) * FPAD, v * EL : (v + 1) * EL] = sign * parts[v]
             outer[f * FPAD : (f + 1) * FPAD, v * EL : (v + 1) * EL] = half * got[v]
     place = 3 * PAD + 6 * FPAD
-    a = dot(operator[:, :place], rhs[...])
-    b = dot(operator[:, 3 * PAD : place], outer[...])
-    count = operator[:, place:]
+    fetches[1].wait()
+    a = dot(table[:, :place], rhs[...])
+    b = dot(table[:, 3 * PAD : place], outer[...])
+    count = table[:, place:]
     lane = lax.broadcasted_iota(jnp.int32, (PAD, EL), 1)
     for v in range(NV):
         uv = u[v]
@@ -278,6 +286,10 @@
 SMEM = pl.BlockSpec(memory_space=pltpu.SMEM)
 
 
+def held(value):
+    return pltpu.with_memory_space_constraint(value, pltpu.HBM)
+
+
 def shifted(value, axis, step):
     count = lax.axis_size(axis)
     return lax.ppermute(value, axis, [(i, (i + step) % count) for i in range(count)])
@@ -287,7 +299,7 @@
     return lax.all_to_all(value, AXES, 0, 0, tiled=True, axis_index_groups=groups)
 
 
-def on_device(state, levels, neighbours, shifts):
+def substep(state, levels, neighbours, shifts):
     planes, columns = plane_groups(), column_groups()
     operator = jnp.asarray(operator_table())
     trace = shape(NV * FPAD, EL)
@@ -300,31 +312,34 @@
         scratch_shapes=[pltpu.VMEM((1, EL), jnp.int32), pltpu.SemaphoreType.DMA((NV + 1,))],
         compiler_params=pltpu.CompilerParams(vmem_limit_bytes=4 << 20),
         name="start",
-    )(pltpu.with_memory_space_constraint(state, pltpu.HBM), pltpu.with_memory_space_constraint(levels, pltpu.HBM))
+    )(held(state), held(levels))
+    peak = exchanged(peak, planes)
     xbelow = shifted(xhi, "slab", 1)
     xabove = shifted(xlo, "slab", -1)
     zbelow = shifted(zhi, "curve", 1)
     zabove = shifted(zlo, "curve", -1)
-    peak = exchanged(peak, planes)
     a, b, to_left, to_right, peak = pl.pallas_call(
         middle_kernel,
         out_shape=(block, block, block, block, shape(len(columns[0]), 1, EL)),
-        in_specs=[VMEM] * 13,
+        in_specs=[VMEM] * 9 + [HBM] + [VMEM] * 2 + [HBM],
         out_specs=(VMEM,) * 5,
         scratch_shapes=[
             pltpu.VMEM((NV * FPAD, EL), jnp.float32),
             pltpu.VMEM((NV * FPAD, EL), jnp.float32),
             pltpu.VMEM((3 * PAD + 6 * FPAD, NV * EL), jnp.float32),
             pltpu.VMEM((6 * FPAD, NV * EL), jnp.float32),
+            pltpu.VMEM((6, 1, EL), jnp.int32),
+            pltpu.VMEM(operator.shape, jnp.float32),
+            pltpu.SemaphoreType.DMA((2,)),
         ],
         compiler_params=pltpu.CompilerParams(vmem_limit_bytes=12 << 20),
         name="middle",
     )(
-        u, xlo, xhi, zlo, zhi, xbelow, xabove, zbelow, zabove, neighbours, scale, peak, operator
+        u, xlo, xhi, zlo, zhi, xbelow, xabove, zbelow, zabove, held(neighbours), scale, peak, held(operator)
     )
+    peak = exchanged(peak, columns)
     from_left = shifted(to_right, "curve", 1)
     from_right = shifted(to_left, "curve", -1)
-    peak = exchanged(peak, columns)
     return pl.pallas_call(
         last_kernel,
         out_shape=(shape(NV, NODES, 1, EL), shape(NV, FACE, 1, EL)),
@@ -348,7 +363,7 @@
         P("slab", "curve"),
     )
     return jax.shard_map(
-        on_device,
+        substep,
         mesh=mesh,
         in_specs=placed,
         out_specs=(P(None, None, "slab", "curve"), P(None, None, "slab", "curve")),

time: 70.7 us -> 69.8 us (0.987)
  local copies, waits for them, and re-layouts: 1.65 us -> 0 us
  Pallas kernels: 5.62 us -> 6.33 us
    unnamed x4 -> x0, local copies, waits for them, and re-layouts: 1.65 us -> none
where the time goes in v2:
time: 69.8 us; the launch traced here: 69.4 us
  starting transfers between devices  40.4 us (58%)
  blocking collectives  12.5 us (18%)
  waiting for transfers between devices  8.74 us (13%)
  Pallas kernels  6.33 us (9%)
  between operations  1.35 us (2%)
    ppermute x6, starting transfers between devices, shifted(): lax.ppermute(value, axis, [(i, (i + step) % count) for i in range(count)])  30.6 us
    all_to_all x1, blocking collectives, exchanged(): lax.all_to_all(value, AXES, 0, 0, tiled=True, axis_index_groups=groups)  12.5 us
    all_to_all x1, starting transfers between devices, exchanged(): lax.all_to_all(value, AXES, 0, 0, tiled=True, axis_index_groups=groups)  9.81 us
    all_to_all x1, waiting for transfers between devices, exchanged(): lax.all_to_all(value, AXES, 0, 0, tiled=True, axis_index_groups=groups)  8.72 us
    pallas_call x1, Pallas kernels, substep(): pl.pallas_call(middle_kernel, out_shape=(block, block, block, block, shap...  3.63 us
    pallas_call x1, Pallas kernels, substep(): pl.pallas_call(last_kernel, out_shape=(shape(NV, NODES, 1, EL), shape(NV,...  1.49 us
  transfers between devices with their start and end apart: 7, of which 1 were waited for; matrix products, arithmetic and copies ran while one was open for 0% of the time, Pallas kernels for 0%

profile of v2, /device:TPU:1, one launch (start us, length us, event | category | flops | bytes accessed | tf_op | source)
XLA Modules:
  0.0 69.4 jit_solution(17622444567425984021)
XLA Ops:
  0.6 1.2 %start.1 = (f32[5,128,128]{2,1,0:T(8,128)S(1)}, f32[1,128]{1,0:T(1,128)S(1)}, f32[32,1,128]{2,1,0:T(1,128)S(1)}, f32[160,128]{1,0:T(8,128)S(1)}, f32[160,128]{1,...) custom-call(f32[5,125,1,128]{3,2,1,0:T(1,128)} %state.1, s32[1,128]{1,0:T(1,128)} %levels.1), custom_call_target="tpu_custom_call" | custom-call | tf_op jit(solution)/shard_map/start/pallas_call | solution.py:307
  1.8 2.6 %collective-permute-start = (f32[160,128]{1,0:T(8,128)S(1)}, f32[160,128]{1,0:T(8,128)S(1)}, u32[]{:S(2)}, u32[]{:S(2)}) collective-permute-start(f32[160,128]{1,0:T(8,128)S(1)} %get-tuple-element.16.xhi), channel_id=1, source_target_pairs={{0,1},{1,2},{2,3},{3,4},{4,5},{5,6},{6,7},{7,0},{8,9},{9,10},{10,1... | collective-permute-start | bytes 245768 | tf_op jit(solution)/shard_map/ppermute | solution.py:295
  4.4 7.9 %collective-permute-start.1 = (f32[160,128]{1,0:T(8,128)S(1)}, f32[160,128]{1,0:T(8,128)S(1)}, u32[]{:S(2)}, u32[]{:S(2)}) collective-permute-start(f32[160,128]{1,0:T(8,128)S(1)} %get-tuple-element.15.xlo), channel_id=1, source_target_pairs={{0,7},{1,0},{2,1},{3,2},{4,3},{5,4},{6,5},{7,6},{8,15},{9,8},{10,9... | collective-permute-start | bytes 245768 | tf_op jit(solution)/shard_map/ppermute | solution.py:295
  12.4 1.9 %collective-permute-start.2 = (f32[160,128]{1,0:T(8,128)S(1)}, f32[160,128]{1,0:T(8,128)S(1)}, u32[]{:S(2)}, u32[]{:S(2)}) collective-permute-start(f32[160,128]{1,0:T(8,128)S(1)} %get-tuple-element.18.zhi), channel_id=1, source_target_pairs={{0,8},{8,16},{16,24},{24,32},{32,40},{40,48},{48,56},{56,64},{64,7... | collective-permute-start | bytes 245768 | tf_op jit(solution)/shard_map/ppermute | solution.py:295
  14.3 9.3 %collective-permute-start.3 = (f32[160,128]{1,0:T(8,128)S(1)}, f32[160,128]{1,0:T(8,128)S(1)}, u32[]{:S(2)}, u32[]{:S(2)}) collective-permute-start(f32[160,128]{1,0:T(8,128)S(1)} %get-tuple-element.17.zlo), channel_id=1, source_target_pairs={{0,760},{8,0},{16,8},{24,16},{32,24},{40,32},{48,40},{56,48},{64,5... | collective-permute-start | bytes 245768 | tf_op jit(solution)/shard_map/ppermute | solution.py:295
  23.6 12.5 %all_to_all.10.peaks = f32[32,1,128]{2,1,0:T(1,128)S(1)} all-to-all(f32[32,1,128]{2,1,0:T(1,128)S(1)} %get-tuple-element.20), channel_id=1, replica_groups={{0,2,4,6,8,10,12,14,16,18,20,22,24,26,28,30,32,34,36,38,40,42,44,46,48,..., dimensions={0} | all-to-all | bytes 32768 | tf_op jit(solution)/shard_map/all_to_all | solution.py:299
  36.1 0.0 collective-permute-done.xbelow
  36.1 0.0 collective-permute-done.1.xabove
  36.1 0.0 collective-permute-done.2.zbelow
  36.1 0.0 collective-permute-done.3.zabove
  36.1 3.6 %middle.1 = (f32[5,128,128]{2,1,0:T(8,128)S(1)}, f32[5,128,128]{2,1,0:T(8,128)S(1)}, f32[5,128,128]{2,1,0:T(8,128)S(1)}, f32[5,128,128]{2,1,0:T(8,128)S(1)}, f32[24,1,128]{2,1,0:T(1,128)}) custom-call(f32[5,128,128]{2,1,0:T(8,128)S(1)} %get-tuple-element.14.u, f32[160,128]{1,0:T(8,128)S(1)} %get-tuple-element.15.xlo, f32[160,128]{1,0:T(8,128)S(1)} %get-tuple-element.16.xhi, ...), custom_call_target="tpu_custom_call" | custom-call | tf_op jit(solution)/shard_map/middle/pallas_call | solution.py:321
  39.8 2.2 %collective-permute-start.4 = (f32[5,128,128]{2,1,0:T(8,128)S(1)}, f32[5,128,128]{2,1,0:T(8,128)S(1)}, u32[]{:S(2)}, u32[]{:S(2)}) collective-permute-start(f32[5,128,128]{2,1,0:T(8,128)S(1)} %get-tuple-element.23), channel_id=1, source_target_pairs={{0,8},{8,16},{16,24},{24,32},{32,40},{40,48},{48,56},{56,64},{64,7... | collective-permute-start | bytes 983048 | tf_op jit(solution)/shard_map/ppermute | solution.py:295
  42.0 6.7 %collective-permute-start.5 = (f32[5,128,128]{2,1,0:T(8,128)S(1)}, f32[5,128,128]{2,1,0:T(8,128)S(1)}, u32[]{:S(2)}, u32[]{:S(2)}) collective-permute-start(f32[5,128,128]{2,1,0:T(8,128)S(1)} %get-tuple-element.24), channel_id=1, source_target_pairs={{0,760},{8,0},{16,8},{24,16},{32,24},{40,32},{48,40},{56,48},{64,5... | collective-permute-start | bytes 983048 | tf_op jit(solution)/shard_map/ppermute | solution.py:295
  48.7 9.8 %all-to-all-start.1 = ((f32[24,1,128]{2,1,0:T(1,128)}), f32[24,1,128]{2,1,0:T(1,128)S(1)}, u32[]{:S(2)}, u32[]{:S(2)}) async-start(f32[24,1,128]{2,1,0:T(1,128)} %get-tuple-element.25), calls=%async_computation.1 | async-start | bytes 24576 | tf_op jit(solution)/shard_map/all_to_all | solution.py:299
  59.2 8.7 %all-to-all-done.1.peaks = f32[24,1,128]{2,1,0:T(1,128)S(1)} async-done(((f32[24,1,128]{2,1,0:T(1,128)}), f32[24,1,128]{2,1,0:T(1,128)S(1)}, u32[]{:S(2)}, u32[]{:S(2)}) %all-to-all-start.1) | async-done | bytes 12320 | tf_op jit(solution)/shard_map/all_to_all | solution.py:299
  67.9 0.0 collective-permute-done.4.from_left
  67.9 0.0 collective-permute-done.5.from_right
  67.9 1.5 %last.1 = (f32[5,125,1,128]{3,2,1,0:T(1,128)}, f32[5,25,1,128]{3,2,1,0:T(1,128)}) custom-call(s32[1,1]{1,0:T(1,128)S(6)} %copy.7.shifts, f32[5,128,128]{2,1,0:T(8,128)S(1)} %get-tuple-element.14.u, f32[5,128,128]{2,1,0:T(8,128)S(1)} %get-tuple-element.21.a, f32[5,128,128]{2,1,0:T(8,128)S(1)} %get-tuple-element.22.b, ...), custom_call_target="tpu_custom_call" | custom-call | tf_op jit(solution)/shard_map/last/pallas_call | solution.py:343
Async XLA Ops:
  1.8 34.3 %collective-permute-start = (f32[160,128]{1,0:T(8,128)S(1)}, f32[160,128]{1,0:T(8,128)S(1)}, u32[]{:S(2)}, u32[]{:S(2)}) collective-permute-start(f32[160,128]{1,0:T(8,128)S(1)} %get-tuple-element.16.xhi), channel_id=1, source_target_pairs={{0,1},{1,2},{2,3},{3,4},{4,5},{5,6},{6,7},{7,0},{8,9},{9,10},{10,1... | collective-permute-start | bytes 245768 | tf_op jit(solution)/shard_map/ppermute | solution.py:295
  4.4 31.7 %collective-permute-start.1 = (f32[160,128]{1,0:T(8,128)S(1)}, f32[160,128]{1,0:T(8,128)S(1)}, u32[]{:S(2)}, u32[]{:S(2)}) collective-permute-start(f32[160,128]{1,0:T(8,128)S(1)} %get-tuple-element.15.xlo), channel_id=1, source_target_pairs={{0,7},{1,0},{2,1},{3,2},{4,3},{5,4},{6,5},{7,6},{8,15},{9,8},{10,9... | collective-permute-start | bytes 245768 | tf_op jit(solution)/shard_map/ppermute | solution.py:295
  12.4 23.8 %collective-permute-start.2 = (f32[160,128]{1,0:T(8,128)S(1)}, f32[160,128]{1,0:T(8,128)S(1)}, u32[]{:S(2)}, u32[]{:S(2)}) collective-permute-start(f32[160,128]{1,0:T(8,128)S(1)} %get-tuple-element.18.zhi), channel_id=1, source_target_pairs={{0,8},{8,16},{16,24},{24,32},{32,40},{40,48},{48,56},{56,64},{64,7... | collective-permute-start | bytes 245768 | tf_op jit(solution)/shard_map/ppermute | solution.py:295
  14.3 21.9 %collective-permute-start.3 = (f32[160,128]{1,0:T(8,128)S(1)}, f32[160,128]{1,0:T(8,128)S(1)}, u32[]{:S(2)}, u32[]{:S(2)}) collective-permute-start(f32[160,128]{1,0:T(8,128)S(1)} %get-tuple-element.17.zlo), channel_id=1, source_target_pairs={{0,760},{8,0},{16,8},{24,16},{32,24},{40,32},{48,40},{56,48},{64,5... | collective-permute-start | bytes 245768 | tf_op jit(solution)/shard_map/ppermute | solution.py:295
  39.8 28.1 %collective-permute-start.4 = (f32[5,128,128]{2,1,0:T(8,128)S(1)}, f32[5,128,128]{2,1,0:T(8,128)S(1)}, u32[]{:S(2)}, u32[]{:S(2)}) collective-permute-start(f32[5,128,128]{2,1,0:T(8,128)S(1)} %get-tuple-element.23), channel_id=1, source_target_pairs={{0,8},{8,16},{16,24},{24,32},{32,40},{40,48},{48,56},{56,64},{64,7... | collective-permute-start | bytes 983048 | tf_op jit(solution)/shard_map/ppermute | solution.py:295
  42.0 25.9 %collective-permute-start.5 = (f32[5,128,128]{2,1,0:T(8,128)S(1)}, f32[5,128,128]{2,1,0:T(8,128)S(1)}, u32[]{:S(2)}, u32[]{:S(2)}) collective-permute-start(f32[5,128,128]{2,1,0:T(8,128)S(1)} %get-tuple-element.24), channel_id=1, source_target_pairs={{0,760},{8,0},{16,8},{24,16},{32,24},{40,32},{48,40},{56,48},{64,5... | collective-permute-start | bytes 983048 | tf_op jit(solution)/shard_map/ppermute | solution.py:295
  48.7 19.2 %all-to-all-start.1 = ((f32[24,1,128]{2,1,0:T(1,128)}), f32[24,1,128]{2,1,0:T(1,128)S(1)}, u32[]{:S(2)}, u32[]{:S(2)}) async-start(f32[24,1,128]{2,1,0:T(1,128)} %get-tuple-element.25), calls=%async_computation.1 | async-start | bytes 24576 | tf_op jit(solution)/shard_map/all_to_all | solution.py:299

commit v3 on v2

--- a/solution.py
+++ b/solution.py
@@ -16,7 +16,9 @@
 END_WEIGHT = 0.1
 PAD = 128
 FPAD = 32
-LANES = 42
+LANES = 32
+SHIFT_MAX = 32
+PACK = NV * PAD // 4
 Z, Y, X, CORES = 12, 8, 4, 2
 HIGH = lax.Precision.HIGHEST
 AXES = ("curve", "slab")
@@ -120,7 +122,34 @@
     return jnp.where(lane < EL // 2, lam, top)
 
 
-def start_kernel(state, levels, u, scale_row, peak, xlo, xhi, zlo, zhi, level, sem):
+def packed(source, out, base, first):
+    lane = lax.broadcasted_iota(jnp.int32, (PACK, EL), 1)
+    total = None
+    for g in range(4):
+        rows, row = [], g * PACK
+        while row < (g + 1) * PACK:
+            v, n = row // PAD, row % PAD
+            size = min(PAD - n, (g + 1) * PACK - row)
+            rows.append(source[v, n : n + size, :])
+            row += size
+        part = pltpu.roll(jnp.concatenate(rows, axis=0), (LANES * g - first) % EL, 1)
+        total = part if g == 0 else jnp.where(lane >= LANES * g, part, total)
+    out[base : base + PACK, :] = total
+
+
+def spread(source, out, base):
+    down = lax.broadcasted_iota(jnp.int32, (FPAD, EL), 0)
+    lane = lax.broadcasted_iota(jnp.int32, (FPAD, EL), 1)
+    for v in range(NV):
+        g, row = divmod(v * PAD + NODES, PACK)
+        column = source[v, PAD - FPAD : PAD, EL - LANES - 1 : EL - LANES]
+        line = jnp.sum(jnp.where(lane - LANES * g == down, column, 0.0), axis=0, keepdims=True)
+        at = slice(base + row, base + row + 1)
+        inside = (lane[:1] >= LANES * g) & (lane[:1] < LANES * (g + 1))
+        out[at, :] = jnp.where(inside, line, out[at, :])
+
+
+def start_kernel(state, levels, u, scale_row, peak, xlo, xhi, down, up, level, sem):
     copies = [
         pltpu.make_async_copy(state.at[v, :, 0], u.at[v, pl.ds(0, NODES)], sem.at[v]) for v in range(NV)
     ]
@@ -150,10 +179,13 @@
         row = v * FPAD
         xlo[row : row + FACE, :] = u[v, pl.ds(0, FACE, stride=5), :]
         xhi[row : row + FACE, :] = u[v, pl.ds(4, FACE, stride=5), :]
-        zlo[row : row + FACE, :] = u[v, 0:FACE, :]
-        zhi[row : row + FACE, :] = u[v, NODES - FACE : NODES, :]
-        for ref in (xlo, xhi, zlo, zhi):
+        down[row : row + FACE, :] = u[v, 0:FACE, :]
+        up[row : row + FACE, :] = u[v, NODES - FACE : NODES, :]
+        for ref in (xlo, xhi, down, up):
             ref[row + FACE : row + FPAD, :] = ones
+    packed(u, down, NV * FPAD, 0)
+    packed(u, up, NV * FPAD, EL - LANES)
+    spread(u, up, NV * FPAD)
 
 
 def dot(a, b):
@@ -161,8 +193,8 @@
 
 
 def middle_kernel(
-    u, xlo, xhi, zlo, zhi, xbelow, xabove, zbelow, zabove, neighbours, scale_row, peaks, operator,
-    a_out, b_out, to_left, to_right, peak, ylo, yhi, rhs, outer, named, table, sem,
+    u, xbelow, xabove, up, down, below, above, neighbours, scale_row, operator,
+    a_out, b_out, to_left, to_right, ylo, yhi, rhs, outer, named, table, sem,
 ):
     fetches = [
         pltpu.make_async_copy(neighbours, named, sem.at[0]),
@@ -170,8 +202,6 @@
     ]
     for fetch in fetches:
         fetch.start()
-    best = jnp.max(peaks[...], axis=0)
-    peak[...] = jnp.broadcast_to(best[None], peak.shape)
     scale = scale_row[...]
     ones = jnp.full((FPAD - FACE, EL), 1.0, jnp.float32)
     for v in range(NV):
@@ -195,11 +225,11 @@
             got = dot(trace[...], (source == offset).astype(jnp.float32))
         else:
             here = (named[f] >> 7) == home
-            mine, other = ((zhi, zbelow), (zlo, zabove))[f - 4]
+            mine, other = ((up, below), (down, above))[f - 4]
             own_index = jnp.where(here, offset, -1)
             other_index = jnp.where(here, -1, offset)
-            got = dot(mine[...], (source == own_index).astype(jnp.float32)) + dot(
-                other[...], (source == other_index).astype(jnp.float32)
+            got = dot(mine[: NV * FPAD], (source == own_index).astype(jnp.float32)) + dot(
+                other[: NV * FPAD], (source == other_index).astype(jnp.float32)
             )
         got = [got[v * FPAD : (v + 1) * FPAD] for v in range(NV)]
         sign = half * (1.0 - 2.0 * (f % 2))
@@ -212,48 +242,52 @@
     a = dot(table[:, :place], rhs[...])
     b = dot(table[:, 3 * PAD : place], outer[...])
     count = table[:, place:]
-    lane = lax.broadcasted_iota(jnp.int32, (PAD, EL), 1)
-    for v in range(NV):
-        uv = u[v]
-        av = a[:, v * EL : (v + 1) * EL] * scale
-        bv = (b[:, v * EL : (v + 1) * EL] - count * uv) * scale
-        a_out[v] = av
-        b_out[v] = bv
-        to_left[v] = jnp.where(
-            lane < LANES,
-            uv,
-            jnp.where(lane < 2 * LANES, pltpu.roll(av, LANES, 1), pltpu.roll(bv, 2 * LANES, 1)),
-        )
-        to_right[v] = jnp.where(
-            lane < LANES,
-            pltpu.roll(uv, LANES, 1),
-            jnp.where(lane < 2 * LANES, pltpu.roll(av, 2 * LANES, 1), pltpu.roll(bv, 3 * LANES, 1)),
-        )
-
-
-def last_kernel(shifts, u, a, b, from_left, from_right, peaks, moved, mortar, new, surface, sem):
+    for v in range(NV):
+        a_out[v] = a[:, v * EL : (v + 1) * EL] * scale
+        b_out[v] = (b[:, v * EL : (v + 1) * EL] - count * u[v]) * scale
+    for i, ref in enumerate((a_out, b_out)):
+        packed(ref, to_left, i * PACK, 0)
+        packed(ref, to_right, i * PACK, EL - LANES)
+        spread(ref, to_right, i * PACK)
+
+
+def merge_kernel(peaks, peak):
+    best = jnp.max(peaks[...], axis=0)
+    peak[...] = jnp.broadcast_to(best[None], peak.shape)
+
+
+def last_kernel(
+    shifts, u, a, b, below, above, from_left, from_right, peaks, moved, mortar, new, surface, halos, sem
+):
     best = jnp.max(peaks[...], axis=0)
     lam = jnp.max(best[:, : EL // 2], axis=1, keepdims=True)
     top = jnp.max(best[:, EL // 2 :], axis=1, keepdims=True)
     step = CFL / top
     shift = shifts[0, 0]
     ahead = shift >= 1
-    turn = jnp.where(ahead, 2 * EL - shift, 2 * EL - shift - LANES) % EL
     own_turn = (2 * EL - shift) % EL
     lane = lax.broadcasted_iota(jnp.int32, (PAD, EL), 1)
     first = jnp.where(ahead, EL - shift, 0)
     end = jnp.where(ahead, EL, -shift)
     outside = (lane >= first) & (lane < end)
+    down = lax.broadcasted_iota(jnp.int32, (FPAD, EL), 0)
     lane_up = lax.broadcasted_iota(jnp.int32, (FPAD, EL), 1)
     outside_up = (lane_up >= jnp.where(ahead, first + 1, 0)) & (lane_up < end + 1)
+    far = lane_up < jnp.where(shift == -SHIFT_MAX, 1, 0)
+    trace = slice(NV * FPAD, NV * FPAD + PACK)
+    pack = jnp.where(ahead, above[trace, :], below[trace, :])
+    rate = jnp.where(ahead, from_right[:PACK], from_left[:PACK]) + lam * jnp.where(
+        ahead, from_right[PACK:], from_left[PACK:]
+    )
+    pack = pack + step * rate
+    back = jnp.where(ahead, 0, LANES) + shift
+    for g in range(4):
+        halos[g * PACK : (g + 1) * PACK, :] = pltpu.roll(pack, (2 * EL - LANES * g - back) % EL, 1)
     low, high = [], []
     copies = []
     for v in range(NV):
-        own = u[v] + step * (a[v] + lam * b[v])
-        pack = jnp.where(ahead, from_right[v], from_left[v])
-        halo = pack + step * (pltpu.roll(pack, EL - LANES, 1) + lam * pltpu.roll(pack, EL - 2 * LANES, 1))
-        own = pltpu.roll(own, own_turn, 1)
-        halo = pltpu.roll(halo, turn, 1)
+        own = pltpu.roll(u[v] + step * (a[v] + lam * b[v]), own_turn, 1)
+        halo = halos[v * PAD : (v + 1) * PAD, :]
         block = jnp.where(outside, halo, own)
         new[v] = block
         copy = pltpu.make_async_copy(new.at[v, pl.ds(0, NODES)], moved.at[v, :, 0], sem.at[v])
@@ -263,6 +297,10 @@
         before = jnp.where(
             outside_up, pltpu.roll(halo[PAD - FPAD :], 1, 1), pltpu.roll(own[PAD - FPAD :], 1, 1)
         )
+        g, row = divmod(v * PAD + NODES, PACK)
+        line = pack[row : row + 1, :]
+        column = jnp.sum(jnp.where(lane_up - LANES * g == down, line, 0.0), axis=1, keepdims=True)
+        before = jnp.where(far, column, before)
         high.append(pltpu.roll(before, FPAD - 4, 0))
     lower, upper = flux(high, 2), flux(low, 2)
     for v in range(NV):
@@ -303,10 +341,12 @@
     planes, columns = plane_groups(), column_groups()
     operator = jnp.asarray(operator_table())
     trace = shape(NV * FPAD, EL)
+    edge = shape(NV * FPAD + PACK, EL)
+    halo = shape(2 * PACK, EL)
     block = shape(NV, PAD, EL)
-    u, scale, peak, xlo, xhi, zlo, zhi = pl.pallas_call(
+    u, scale, peak, xlo, xhi, down, up = pl.pallas_call(
         start_kernel,
-        out_shape=(block, shape(1, EL), shape(len(planes[0]), 1, EL), trace, trace, trace, trace),
+        out_shape=(block, shape(1, EL), shape(len(planes[0]), 1, EL), trace, trace, edge, edge),
         in_specs=[HBM, HBM],
         out_specs=(VMEM,) * 7,
         scratch_shapes=[pltpu.VMEM((1, EL), jnp.int32), pltpu.SemaphoreType.DMA((NV + 1,))],
@@ -316,13 +356,13 @@
     peak = exchanged(peak, planes)
     xbelow = shifted(xhi, "slab", 1)
     xabove = shifted(xlo, "slab", -1)
-    zbelow = shifted(zhi, "curve", 1)
-    zabove = shifted(zlo, "curve", -1)
-    a, b, to_left, to_right, peak = pl.pallas_call(
+    below = shifted(up, "curve", 1)
+    above = shifted(down, "curve", -1)
+    a, b, to_left, to_right = pl.pallas_call(
         middle_kernel,
-        out_shape=(block, block, block, block, shape(len(columns[0]), 1, EL)),
-        in_specs=[VMEM] * 9 + [HBM] + [VMEM] * 2 + [HBM],
-        out_specs=(VMEM,) * 5,
+        out_shape=(block, block, halo, halo),
+        in_specs=[VMEM] * 7 + [HBM, VMEM, HBM],
+        out_specs=(VMEM,) * 4,
         scratch_shapes=[
             pltpu.VMEM((NV * FPAD, EL), jnp.float32),
             pltpu.VMEM((NV * FPAD, EL), jnp.float32),
@@ -335,24 +375,33 @@
         compiler_params=pltpu.CompilerParams(vmem_limit_bytes=12 << 20),
         name="middle",
     )(
-        u, xlo, xhi, zlo, zhi, xbelow, xabove, zbelow, zabove, held(neighbours), scale, peak, held(operator)
+        u, xbelow, xabove, up, down, below, above, held(neighbours), scale, held(operator)
     )
+    peak = pl.pallas_call(
+        merge_kernel,
+        out_shape=shape(len(columns[0]), 1, EL),
+        in_specs=[VMEM],
+        out_specs=VMEM,
+        compiler_params=pltpu.CompilerParams(vmem_limit_bytes=1 << 20),
+        name="merge",
+    )(peak)
     peak = exchanged(peak, columns)
     from_left = shifted(to_right, "curve", 1)
     from_right = shifted(to_left, "curve", -1)
     return pl.pallas_call(
         last_kernel,
         out_shape=(shape(NV, NODES, 1, EL), shape(NV, FACE, 1, EL)),
-        in_specs=[SMEM] + [VMEM] * 6,
+        in_specs=[SMEM] + [VMEM] * 8,
         out_specs=(ANY, ANY),
         scratch_shapes=[
             pltpu.VMEM((NV, PAD, EL), jnp.float32),
             pltpu.VMEM((NV, FPAD, EL), jnp.float32),
+            pltpu.VMEM((NV * PAD, EL), jnp.float32),
             pltpu.SemaphoreType.DMA((2 * NV,)),
         ],
         compiler_params=pltpu.CompilerParams(vmem_limit_bytes=8 << 20),
         name="last",
-    )(shifts, u, a, b, from_left, from_right, peak)
+    )(shifts, u, a, b, below, above, from_left, from_right, peak)
 
 
 def solution(mesh):

time: 69.8 us -> 71.1 us (1.019)
  waiting for transfers between devices: 8.74 us -> 12.6 us
  starting transfers between devices: 40.4 us -> 37.6 us
    ppermute x6, waiting for transfers between devices: 0.02 us -> 3.87 us  [shifted(): lax.ppermute(value, axis, [(i, (i + step) % count) for i in range(count)])]
    all_to_all x1, starting transfers between devices: 9.81 us -> 6.95 us  [exchanged(): lax.all_to_all(value, AXES, 0, 0, tiled=True, axis_index_groups=groups)]
    pallas_call x1 -> x2, Pallas kernels: 3.63 us -> 3.7 us  [the longest x1 3.08 us: substep(): pl.pallas_call(middle_kernel, out_shape=(block, block, halo, halo), in_sp...]
  transfers between devices with their start and end apart: 7 -> 7, of which waited for: 1 -> 3; matrix products, arithmetic and copies ran while one was open for 0% -> 0% of each run, Pallas kernels for 0% -> 1%
where the time goes in v3:
time: 71.1 us; the launch traced here: 70.7 us
  starting transfers between devices  37.6 us (53%)
  blocking collectives  12.8 us (18%)
  waiting for transfers between devices  12.6 us (18%)
  Pallas kernels  6.43 us (9%)
  between operations  1.34 us (2%)
    ppermute x6, starting transfers between devices, shifted(): lax.ppermute(value, axis, [(i, (i + step) % count) for i in range(count)])  30.6 us
    all_to_all x1, blocking collectives, exchanged(): lax.all_to_all(value, AXES, 0, 0, tiled=True, axis_index_groups=groups)  12.8 us
    all_to_all x1, waiting for transfers between devices, exchanged(): lax.all_to_all(value, AXES, 0, 0, tiled=True, axis_index_groups=groups)  8.72 us
    all_to_all x1, starting transfers between devices, exchanged(): lax.all_to_all(value, AXES, 0, 0, tiled=True, axis_index_groups=groups)  6.95 us
    ppermute x6, waiting for transfers between devices, shifted(): lax.ppermute(value, axis, [(i, (i + step) % count) for i in range(count)])  3.87 us
    pallas_call x1, Pallas kernels, substep(): pl.pallas_call(middle_kernel, out_shape=(block, block, halo, halo), in_sp...  3.08 us
  transfers between devices with their start and end apart: 7, of which 3 were waited for; matrix products, arithmetic and copies ran while one was open for 0% of the time, Pallas kernels for 1%

profile of v3, /device:TPU:1, one launch (start us, length us, event | category | flops | bytes accessed | tf_op | source)
XLA Modules:
  0.0 70.7 jit_solution(2855959871537244997)
XLA Ops:
  0.6 1.3 %start.1 = (f32[5,128,128]{2,1,0:T(8,128)S(1)}, f32[1,128]{1,0:T(1,128)S(1)}, f32[32,1,128]{2,1,0:T(1,128)S(1)}, f32[160,128]{1,0:T(8,128)S(1)}, f32[160,128]{1,...) custom-call(f32[5,125,1,128]{3,2,1,0:T(1,128)} %state.1, s32[1,128]{1,0:T(1,128)} %levels.1), custom_call_target="tpu_custom_call" | custom-call | tf_op jit(solution)/shard_map/start/pallas_call | solution.py:347
  2.0 4.0 %collective-permute-start.2 = (f32[320,128]{1,0:T(8,128)S(1)}, f32[320,128]{1,0:T(8,128)S(1)}, u32[]{:S(2)}, u32[]{:S(2)}) collective-permute-start(f32[320,128]{1,0:T(8,128)S(1)} %get-tuple-element.16.up), channel_id=1, source_target_pairs={{0,8},{8,16},{16,24},{24,32},{32,40},{40,48},{48,56},{56,64},{64,7... | collective-permute-start | bytes 491528 | tf_op jit(solution)/shard_map/ppermute | solution.py:333
  6.0 15.9 %collective-permute-start.3 = (f32[320,128]{1,0:T(8,128)S(1)}, f32[320,128]{1,0:T(8,128)S(1)}, u32[]{:S(2)}, u32[]{:S(2)}) collective-permute-start(f32[320,128]{1,0:T(8,128)S(1)} %get-tuple-element.17.down), channel_id=1, source_target_pairs={{0,760},{8,0},{16,8},{24,16},{32,24},{40,32},{48,40},{56,48},{64,5... | collective-permute-start | bytes 491528 | tf_op jit(solution)/shard_map/ppermute | solution.py:333
  21.9 2.1 %collective-permute-start = (f32[160,128]{1,0:T(8,128)S(1)}, f32[160,128]{1,0:T(8,128)S(1)}, u32[]{:S(2)}, u32[]{:S(2)}) collective-permute-start(f32[160,128]{1,0:T(8,128)S(1)} %get-tuple-element.14), channel_id=1, source_target_pairs={{0,1},{1,2},{2,3},{3,4},{4,5},{5,6},{6,7},{7,0},{8,9},{9,10},{10,1... | collective-permute-start | bytes 245768 | tf_op jit(solution)/shard_map/ppermute | solution.py:333
  24.0 0.0 collective-permute-start.1
  24.0 1.5 %collective-permute-done.xbelow = f32[160,128]{1,0:T(8,128)S(1)} collective-permute-done((f32[160,128]{1,0:T(8,128)S(1)}, f32[160,128]{1,0:T(8,128)S(1)}, u32[]{:S(2)}, u32[]{:S(2)}) %collective-permute-start) | collective-permute-done | bytes 81952 | tf_op jit(solution)/shard_map/ppermute | solution.py:333
  25.5 2.4 %collective-permute-done.1.xabove = f32[160,128]{1,0:T(8,128)S(1)} collective-permute-done((f32[160,128]{1,0:T(8,128)S(1)}, f32[160,128]{1,0:T(8,128)S(1)}, u32[]{:S(2)}, u32[]{:S(2)}) %collective-permute-start.1) | collective-permute-done | bytes 81952 | tf_op jit(solution)/shard_map/ppermute | solution.py:333
  27.9 0.0 collective-permute-done.2.below
  27.9 0.0 collective-permute-done.3.above
  27.9 3.1 %middle.1 = (f32[5,128,128]{2,1,0:T(8,128)S(1)}, f32[5,128,128]{2,1,0:T(8,128)S(1)}, f32[320,128]{1,0:T(8,128)S(1)}, f32[320,128]{1,0:T(8,128)S(1)}) custom-call(f32[5,128,128]{2,1,0:T(8,128)S(1)} %get-tuple-element.13.u, f32[160,128]{1,0:T(8,128)S(1)} %collective-permute-done.xbelow, f32[160,128]{1,0:T(8,128)S(1)} %collective-permute-done.1.xabove, ...), custom_call_target="tpu_custom_call" | custom-call | tf_op jit(solution)/shard_map/middle/pallas_call | solution.py:361
  31.0 1.9 %collective-permute-start.4 = (f32[320,128]{1,0:T(8,128)S(1)}, f32[320,128]{1,0:T(8,128)S(1)}, u32[]{:S(2)}, u32[]{:S(2)}) collective-permute-start(f32[320,128]{1,0:T(8,128)S(1)} %get-tuple-element.21), channel_id=1, source_target_pairs={{0,8},{8,16},{16,24},{24,32},{32,40},{40,48},{48,56},{56,64},{64,7... | collective-permute-start | bytes 491528 | tf_op jit(solution)/shard_map/ppermute | solution.py:333
  32.9 6.7 %collective-permute-start.5 = (f32[320,128]{1,0:T(8,128)S(1)}, f32[320,128]{1,0:T(8,128)S(1)}, u32[]{:S(2)}, u32[]{:S(2)}) collective-permute-start(f32[320,128]{1,0:T(8,128)S(1)} %get-tuple-element.22), channel_id=1, source_target_pairs={{0,760},{8,0},{16,8},{24,16},{32,24},{40,32},{48,40},{56,48},{64,5... | collective-permute-start | bytes 491528 | tf_op jit(solution)/shard_map/ppermute | solution.py:333
  39.6 12.8 %all_to_all.10.peaks = f32[32,1,128]{2,1,0:T(1,128)S(1)} all-to-all(f32[32,1,128]{2,1,0:T(1,128)S(1)} %get-tuple-element.23), channel_id=1, replica_groups={{0,2,4,6,8,10,12,14,16,18,20,22,24,26,28,30,32,34,36,38,40,42,44,46,48,..., dimensions={0} | all-to-all | bytes 32768 | tf_op jit(solution)/shard_map/all_to_all | solution.py:337
  52.3 0.6 merge.1
  53.0 7.0 %all-to-all-start.1 = ((f32[24,1,128]{2,1,0:T(1,128)}), f32[24,1,128]{2,1,0:T(1,128)S(1)}, u32[]{:S(2)}, u32[]{:S(2)}) async-start(f32[24,1,128]{2,1,0:T(1,128)} %merge.1), calls=%async_computation.1 | async-start | bytes 24576 | tf_op jit(solution)/shard_map/all_to_all | solution.py:337
  60.6 8.7 %all-to-all-done.1.peaks = f32[24,1,128]{2,1,0:T(1,128)S(1)} async-done(((f32[24,1,128]{2,1,0:T(1,128)}), f32[24,1,128]{2,1,0:T(1,128)S(1)}, u32[]{:S(2)}, u32[]{:S(2)}) %all-to-all-start.1) | async-done | bytes 12320 | tf_op jit(solution)/shard_map/all_to_all | solution.py:337
  69.3 0.0 collective-permute-done.4.from_left
  69.3 0.0 collective-permute-done.5.from_right
  69.3 1.4 %last.1 = (f32[5,125,1,128]{3,2,1,0:T(1,128)}, f32[5,25,1,128]{3,2,1,0:T(1,128)}) custom-call(s32[1,1]{1,0:T(1,128)S(6)} %copy.7.shifts, f32[5,128,128]{2,1,0:T(8,128)S(1)} %get-tuple-element.13.u, f32[5,128,128]{2,1,0:T(8,128)S(1)} %get-tuple-element.19.a, f32[5,128,128]{2,1,0:T(8,128)S(1)} %get-tuple-element.20.b, ...), custom_call_target="tpu_custom_call" | custom-call | tf_op jit(solution)/shard_map/last/pallas_call | solution.py:391
Async XLA Ops:
  2.0 25.9 %collective-permute-start.2 = (f32[320,128]{1,0:T(8,128)S(1)}, f32[320,128]{1,0:T(8,128)S(1)}, u32[]{:S(2)}, u32[]{:S(2)}) collective-permute-start(f32[320,128]{1,0:T(8,128)S(1)} %get-tuple-element.16.up), channel_id=1, source_target_pairs={{0,8},{8,16},{16,24},{24,32},{32,40},{40,48},{48,56},{56,64},{64,7... | collective-permute-start | bytes 491528 | tf_op jit(solution)/shard_map/ppermute | solution.py:333
  6.0 21.9 %collective-permute-start.3 = (f32[320,128]{1,0:T(8,128)S(1)}, f32[320,128]{1,0:T(8,128)S(1)}, u32[]{:S(2)}, u32[]{:S(2)}) collective-permute-start(f32[320,128]{1,0:T(8,128)S(1)} %get-tuple-element.17.down), channel_id=1, source_target_pairs={{0,760},{8,0},{16,8},{24,16},{32,24},{40,32},{48,40},{56,48},{64,5... | collective-permute-start | bytes 491528 | tf_op jit(solution)/shard_map/ppermute | solution.py:333
  21.9 3.5 %collective-permute-start = (f32[160,128]{1,0:T(8,128)S(1)}, f32[160,128]{1,0:T(8,128)S(1)}, u32[]{:S(2)}, u32[]{:S(2)}) collective-permute-start(f32[160,128]{1,0:T(8,128)S(1)} %get-tuple-element.14), channel_id=1, source_target_pairs={{0,1},{1,2},{2,3},{3,4},{4,5},{5,6},{6,7},{7,0},{8,9},{9,10},{10,1... | collective-permute-start | bytes 245768 | tf_op jit(solution)/shard_map/ppermute | solution.py:333
  24.0 3.9 %collective-permute-start.1 = (f32[160,128]{1,0:T(8,128)S(1)}, f32[160,128]{1,0:T(8,128)S(1)}, u32[]{:S(2)}, u32[]{:S(2)}) collective-permute-start(f32[160,128]{1,0:T(8,128)S(1)} %get-tuple-element.15), channel_id=1, source_target_pairs={{0,7},{1,0},{2,1},{3,2},{4,3},{5,4},{6,5},{7,6},{8,15},{9,8},{10,9... | collective-permute-start | bytes 245768 | tf_op jit(solution)/shard_map/ppermute | solution.py:333
  31.0 38.3 %collective-permute-start.4 = (f32[320,128]{1,0:T(8,128)S(1)}, f32[320,128]{1,0:T(8,128)S(1)}, u32[]{:S(2)}, u32[]{:S(2)}) collective-permute-start(f32[320,128]{1,0:T(8,128)S(1)} %get-tuple-element.21), channel_id=1, source_target_pairs={{0,8},{8,16},{16,24},{24,32},{32,40},{40,48},{48,56},{56,64},{64,7... | collective-permute-start | bytes 491528 | tf_op jit(solution)/shard_map/ppermute | solution.py:333
  32.9 36.4 %collective-permute-start.5 = (f32[320,128]{1,0:T(8,128)S(1)}, f32[320,128]{1,0:T(8,128)S(1)}, u32[]{:S(2)}, u32[]{:S(2)}) collective-permute-start(f32[320,128]{1,0:T(8,128)S(1)} %get-tuple-element.22), channel_id=1, source_target_pairs={{0,760},{8,0},{16,8},{24,16},{32,24},{40,32},{48,40},{56,48},{64,5... | collective-permute-start | bytes 491528 | tf_op jit(solution)/shard_map/ppermute | solution.py:333
  53.0 16.3 %all-to-all-start.1 = ((f32[24,1,128]{2,1,0:T(1,128)}), f32[24,1,128]{2,1,0:T(1,128)S(1)}, u32[]{:S(2)}, u32[]{:S(2)}) async-start(f32[24,1,128]{2,1,0:T(1,128)} %merge.1), calls=%async_computation.1 | async-start | bytes 24576 | tf_op jit(solution)/shard_map/all_to_all | solution.py:337

commit v4 on v3

--- a/solution.py
+++ b/solution.py
@@ -20,7 +20,6 @@
 SHIFT_MAX = 32
 PACK = NV * PAD // 4
 Z, Y, X, CORES = 12, 8, 4, 2
-HIGH = lax.Precision.HIGHEST
 AXES = ("curve", "slab")
 
 
@@ -73,14 +72,15 @@
         full = np.kron(parts[0], np.kron(parts[1], parts[2]))
         volume[:NODES, d * PAD : d * PAD + NODES] = -full
     place = np.zeros((PAD, 6 * FPAD))
-    count = np.zeros((PAD, 1))
     for f in range(6):
         sign = 1.0 - 2.0 * (f % 2)
         for m, n in enumerate(face_nodes(f)):
             place[n, f * FPAD + m] = 1.0
             volume[n, (f // 2) * PAD + n] -= sign * half
-            count[n, 0] += half
-    return np.concatenate([volume, place, np.broadcast_to(count, (PAD, EL))], axis=1).astype(np.float32)
+    top = volume.astype(jnp.bfloat16)
+    rest = (volume - top.astype(np.float64)).astype(jnp.bfloat16)
+    place = place.astype(jnp.bfloat16)
+    return np.concatenate([np.concatenate([top, place], axis=1), np.concatenate([rest, place], axis=1)])
 
 
 def flux(u, d):
@@ -149,7 +149,7 @@
         out[at, :] = jnp.where(inside, line, out[at, :])
 
 
-def start_kernel(state, levels, u, scale_row, peak, xlo, xhi, down, up, level, sem):
+def start_kernel(state, levels, u, scale_row, peak, xlo, xhi, down, up, level, best, sem):
     copies = [
         pltpu.make_async_copy(state.at[v, :, 0], u.at[v, pl.ds(0, NODES)], sem.at[v]) for v in range(NV)
     ]
@@ -173,7 +173,9 @@
     speed = jnp.max(speed, axis=0, keepdims=True)
     lam = jnp.max(speed, axis=1, keepdims=True)
     top = jnp.max(speed * scale, axis=1, keepdims=True)
-    peak[...] = jnp.broadcast_to(lane_pair(lam, top)[None], peak.shape)
+    best[...] = jnp.broadcast_to(lane_pair(lam, top)[None], best.shape)
+    send = pltpu.make_async_copy(best, peak, sem.at[NV + 1])
+    send.start()
     ones = jnp.full((FPAD - FACE, EL), 1.0, jnp.float32)
     for v in range(NV):
         row = v * FPAD
@@ -186,15 +188,25 @@
     packed(u, down, NV * FPAD, 0)
     packed(u, up, NV * FPAD, EL - LANES)
     spread(u, up, NV * FPAD)
+    send.wait()
 
 
 def dot(a, b):
-    return jnp.dot(a, b, precision=HIGH, preferred_element_type=jnp.float32)
+    return jnp.dot(a, b, preferred_element_type=jnp.float32)
+
+
+def halves(value):
+    top = value.astype(jnp.bfloat16)
+    return top, (value - top.astype(jnp.float32)).astype(jnp.bfloat16)
+
+
+def chosen(trace, pick):
+    return jnp.take_along_axis(trace, jnp.broadcast_to(pick, trace.shape), axis=1, mode="promise_in_bounds")
 
 
 def middle_kernel(
-    u, xbelow, xabove, up, down, below, above, neighbours, scale_row, operator,
-    a_out, b_out, to_left, to_right, ylo, yhi, rhs, outer, named, table, sem,
+    u, xlo, xhi, xbelow, xabove, up, down, below, above, neighbours, scale_row, operator,
+    a_out, b_out, to_left, to_right, ylo, yhi, rhs_top, rhs_rest, out_top, out_rest, named, table, sem,
 ):
     fetches = [
         pltpu.make_async_copy(neighbours, named, sem.at[0]),
@@ -211,40 +223,43 @@
             yhi[row + 5 * k : row + 5 * k + 5, :] = u[v, 25 * k + 20 : 25 * k + 25, :]
         ylo[row + FACE : row + FPAD, :] = ones
         yhi[row + FACE : row + FPAD, :] = ones
+
     for d, parts in enumerate(all_fluxes([u[v] for v in range(NV)])):
         for v in range(NV):
-            rhs[d * PAD : (d + 1) * PAD, v * EL : (v + 1) * EL] = parts[v]
-    source = lax.broadcasted_iota(jnp.int32, (EL, EL), 0)
+            at = (slice(d * PAD, (d + 1) * PAD), slice(v * EL, (v + 1) * EL))
+            rhs_top[at], rhs_rest[at] = halves(parts[v])
     fetches[0].wait()
     home = named[2] >> 7
     half = 0.5 / END_WEIGHT
+    nodes = NV * FPAD
     for f in range(6):
         offset = named[f] & (EL - 1)
+        own = (xlo, xhi, ylo, yhi, down, up)[f]
         if f < 4:
-            trace = (xbelow, xabove, yhi, ylo)[f]
-            got = dot(trace[...], (source == offset).astype(jnp.float32))
+            got = chosen((xbelow, xabove, yhi, ylo)[f][...], offset)
         else:
+            pick = offset
+            mine, other = ((up, below), (down, above))[f - 4]
             here = (named[f] >> 7) == home
-            mine, other = ((up, below), (down, above))[f - 4]
-            own_index = jnp.where(here, offset, -1)
-            other_index = jnp.where(here, -1, offset)
-            got = dot(mine[: NV * FPAD], (source == own_index).astype(jnp.float32)) + dot(
-                other[: NV * FPAD], (source == other_index).astype(jnp.float32)
-            )
-        got = [got[v * FPAD : (v + 1) * FPAD] for v in range(NV)]
+            got = jnp.where(here, chosen(mine[:nodes], pick), chosen(other[:nodes], pick))
         sign = half * (1.0 - 2.0 * (f % 2))
-        parts = flux(got, f // 2)
+        values = [got[v * FPAD : (v + 1) * FPAD] for v in range(NV)]
+        parts = flux(values, f // 2)
+        rows = slice(f * FPAD, (f + 1) * FPAD)
         for v in range(NV):
-            rhs[3 * PAD + f * FPAD : 3 * PAD + (f + 1) * FPAD, v * EL : (v + 1) * EL] = sign * parts[v]
-            outer[f * FPAD : (f + 1) * FPAD, v * EL : (v + 1) * EL] = half * got[v]
-    place = 3 * PAD + 6 * FPAD
+            lanes = slice(v * EL, (v + 1) * EL)
+            at = (slice(3 * PAD + f * FPAD, 3 * PAD + (f + 1) * FPAD), lanes)
+            rhs_top[at], rhs_rest[at] = halves(sign * parts[v])
+            jump = half * (values[v] - own[v * FPAD : (v + 1) * FPAD, :])
+            out_top[rows, lanes], out_rest[rows, lanes] = halves(jump)
     fetches[1].wait()
-    a = dot(table[:, :place], rhs[...])
-    b = dot(table[:, 3 * PAD : place], outer[...])
-    count = table[:, place:]
+    first = dot(table[...][:, : 3 * PAD], rhs_top[: 3 * PAD, :])
+    a = first[:PAD] + first[PAD:] + dot(table[:PAD, :], rhs_rest[...])
+    a = a + dot(table[:PAD, 3 * PAD :], rhs_top[3 * PAD :, :])
+    b = dot(table[:PAD, 3 * PAD :], out_top[...]) + dot(table[:PAD, 3 * PAD :], out_rest[...])
     for v in range(NV):
         a_out[v] = a[:, v * EL : (v + 1) * EL] * scale
-        b_out[v] = (b[:, v * EL : (v + 1) * EL] - count * u[v]) * scale
+        b_out[v] = b[:, v * EL : (v + 1) * EL] * scale
     for i, ref in enumerate((a_out, b_out)):
         packed(ref, to_left, i * PACK, 0)
         packed(ref, to_right, i * PACK, EL - LANES)
@@ -338,7 +353,7 @@
 
 
 def substep(state, levels, neighbours, shifts):
-    planes, columns = plane_groups(), column_groups()
+    planes, columns = column_groups(), plane_groups()
     operator = jnp.asarray(operator_table())
     trace = shape(NV * FPAD, EL)
     edge = shape(NV * FPAD + PACK, EL)
@@ -348,8 +363,12 @@
         start_kernel,
         out_shape=(block, shape(1, EL), shape(len(planes[0]), 1, EL), trace, trace, edge, edge),
         in_specs=[HBM, HBM],
-        out_specs=(VMEM,) * 7,
-        scratch_shapes=[pltpu.VMEM((1, EL), jnp.int32), pltpu.SemaphoreType.DMA((NV + 1,))],
+        out_specs=(VMEM, VMEM, HBM) + (VMEM,) * 4,
+        scratch_shapes=[
+            pltpu.VMEM((1, EL), jnp.int32),
+            pltpu.VMEM((len(planes[0]), 1, EL), jnp.float32),
+            pltpu.SemaphoreType.DMA((NV + 2,)),
+        ],
         compiler_params=pltpu.CompilerParams(vmem_limit_bytes=4 << 20),
         name="start",
     )(held(state), held(levels))
@@ -361,21 +380,23 @@
     a, b, to_left, to_right = pl.pallas_call(
         middle_kernel,
         out_shape=(block, block, halo, halo),
-        in_specs=[VMEM] * 7 + [HBM, VMEM, HBM],
+        in_specs=[VMEM] * 9 + [HBM, VMEM, HBM],
         out_specs=(VMEM,) * 4,
         scratch_shapes=[
             pltpu.VMEM((NV * FPAD, EL), jnp.float32),
             pltpu.VMEM((NV * FPAD, EL), jnp.float32),
-            pltpu.VMEM((3 * PAD + 6 * FPAD, NV * EL), jnp.float32),
-            pltpu.VMEM((6 * FPAD, NV * EL), jnp.float32),
+            pltpu.VMEM((3 * PAD + 6 * FPAD, NV * EL), jnp.bfloat16),
+            pltpu.VMEM((3 * PAD + 6 * FPAD, NV * EL), jnp.bfloat16),
+            pltpu.VMEM((6 * FPAD, NV * EL), jnp.bfloat16),
+            pltpu.VMEM((6 * FPAD, NV * EL), jnp.bfloat16),
             pltpu.VMEM((6, 1, EL), jnp.int32),
-            pltpu.VMEM(operator.shape, jnp.float32),
+            pltpu.VMEM(operator.shape, jnp.bfloat16),
             pltpu.SemaphoreType.DMA((2,)),
         ],
         compiler_params=pltpu.CompilerParams(vmem_limit_bytes=12 << 20),
         name="middle",
     )(
-        u, xbelow, xabove, up, down, below, above, held(neighbours), scale, held(operator)
+        u, xlo, xhi, xbelow, xabove, up, down, below, above, held(neighbours), scale, held(operator)
     )
     peak = pl.pallas_call(
         merge_kernel,

time: 71.1 us -> 69.1 us (0.972)
  Pallas kernels: 6.43 us -> 5.37 us
  starting transfers between devices: 37.6 us -> 36.6 us
  blocking collectives: 12.8 us -> 13.7 us
  waiting for transfers between devices: 12.6 us -> 11.8 us
    pallas_call x1, Pallas kernels: 3.08 us -> 1.91 us  [substep(): pl.pallas_call(middle_kernel, out_shape=(block, block, halo, halo), in_sp...]
    all_to_all x1, starting transfers between devices: 6.95 us -> 6.02 us  [exchanged(): lax.all_to_all(value, AXES, 0, 0, tiled=True, axis_index_groups=groups)]
    all_to_all x1, blocking collectives: 12.8 us -> 13.7 us  [exchanged(): lax.all_to_all(value, AXES, 0, 0, tiled=True, axis_index_groups=groups)]
    all_to_all x1, waiting for transfers between devices: 8.72 us -> 7.89 us  [exchanged(): lax.all_to_all(value, AXES, 0, 0, tiled=True, axis_index_groups=groups)]
where the time goes in v4:
time: 69.1 us; the launch traced here: 68.8 us
  starting transfers between devices  36.6 us (53%)
  blocking collectives  13.7 us (20%)
  waiting for transfers between devices  11.8 us (17%)
  Pallas kernels  5.37 us (8%)
  between operations  1.34 us (2%)
    ppermute x6, starting transfers between devices, shifted(): lax.ppermute(value, axis, [(i, (i + step) % count) for i in range(count)])  30.6 us
    all_to_all x1, blocking collectives, exchanged(): lax.all_to_all(value, AXES, 0, 0, tiled=True, axis_index_groups=groups)  13.7 us
    all_to_all x1, waiting for transfers between devices, exchanged(): lax.all_to_all(value, AXES, 0, 0, tiled=True, axis_index_groups=groups)  7.89 us
    all_to_all x1, starting transfers between devices, exchanged(): lax.all_to_all(value, AXES, 0, 0, tiled=True, axis_index_groups=groups)  6.02 us
    ppermute x6, waiting for transfers between devices, shifted(): lax.ppermute(value, axis, [(i, (i + step) % count) for i in range(count)])  3.87 us
    pallas_call x1, Pallas kernels, substep(): pl.pallas_call(middle_kernel, out_shape=(block, block, halo, halo), in_sp...  1.91 us
    pallas_call x1, Pallas kernels, substep(): pl.pallas_call(start_kernel, out_shape=(block, shape(1, EL), shape(len(pl...  1.44 us
    pallas_call x1, Pallas kernels, substep(): pl.pallas_call(last_kernel, out_shape=(shape(NV, NODES, 1, EL), shape(NV,...  1.39 us
  transfers between devices with their start and end apart: 7, of which 3 were waited for; matrix products, arithmetic and copies ran while one was open for 0% of the time, Pallas kernels for 1%

profile of v4, /device:TPU:1, one launch (start us, length us, event | category | flops | bytes accessed | tf_op | source)
XLA Modules:
  0.0 68.8 jit_solution(15634673270837701784)
XLA Ops:
  0.6 1.4 %start.1 = (f32[5,128,128]{2,1,0:T(8,128)S(1)}, f32[1,128]{1,0:T(1,128)S(1)}, f32[24,1,128]{2,1,0:T(1,128)S(1)}, f32[160,128]{1,0:T(8,128)S(1)}, f32[160,128]{1,...) custom-call(f32[5,125,1,128]{3,2,1,0:T(1,128)} %state.1, s32[1,128]{1,0:T(1,128)} %levels.1), custom_call_target="tpu_custom_call" | custom-call | tf_op jit(solution)/shard_map/start/pallas_call | solution.py:362
  2.1 4.0 %collective-permute-start.2 = (f32[320,128]{1,0:T(8,128)S(1)}, f32[320,128]{1,0:T(8,128)S(1)}, u32[]{:S(2)}, u32[]{:S(2)}) collective-permute-start(f32[320,128]{1,0:T(8,128)S(1)} %get-tuple-element.16.up), channel_id=1, source_target_pairs={{0,8},{8,16},{16,24},{24,32},{32,40},{40,48},{48,56},{56,64},{64,7... | collective-permute-start | bytes 491528 | tf_op jit(solution)/shard_map/ppermute | solution.py:348
  6.1 15.9 %collective-permute-start.3 = (f32[320,128]{1,0:T(8,128)S(1)}, f32[320,128]{1,0:T(8,128)S(1)}, u32[]{:S(2)}, u32[]{:S(2)}) collective-permute-start(f32[320,128]{1,0:T(8,128)S(1)} %get-tuple-element.17.down), channel_id=1, source_target_pairs={{0,760},{8,0},{16,8},{24,16},{32,24},{40,32},{48,40},{56,48},{64,5... | collective-permute-start | bytes 491528 | tf_op jit(solution)/shard_map/ppermute | solution.py:348
  22.0 2.1 %collective-permute-start = (f32[160,128]{1,0:T(8,128)S(1)}, f32[160,128]{1,0:T(8,128)S(1)}, u32[]{:S(2)}, u32[]{:S(2)}) collective-permute-start(f32[160,128]{1,0:T(8,128)S(1)} %get-tuple-element.15.xhi), channel_id=1, source_target_pairs={{0,1},{1,2},{2,3},{3,4},{4,5},{5,6},{6,7},{7,0},{8,9},{9,10},{10,1... | collective-permute-start | bytes 245768 | tf_op jit(solution)/shard_map/ppermute | solution.py:348
  24.1 0.0 collective-permute-start.1
  24.1 1.5 %collective-permute-done.xbelow = f32[160,128]{1,0:T(8,128)S(1)} collective-permute-done((f32[160,128]{1,0:T(8,128)S(1)}, f32[160,128]{1,0:T(8,128)S(1)}, u32[]{:S(2)}, u32[]{:S(2)}) %collective-permute-start) | collective-permute-done | bytes 81952 | tf_op jit(solution)/shard_map/ppermute | solution.py:348
  25.6 2.4 %collective-permute-done.1.xabove = f32[160,128]{1,0:T(8,128)S(1)} collective-permute-done((f32[160,128]{1,0:T(8,128)S(1)}, f32[160,128]{1,0:T(8,128)S(1)}, u32[]{:S(2)}, u32[]{:S(2)}) %collective-permute-start.1) | collective-permute-done | bytes 81952 | tf_op jit(solution)/shard_map/ppermute | solution.py:348
  28.0 0.0 collective-permute-done.2.below
  28.0 0.0 collective-permute-done.3.above
  28.0 1.9 %middle.1 = (f32[5,128,128]{2,1,0:T(8,128)S(1)}, f32[5,128,128]{2,1,0:T(8,128)S(1)}, f32[320,128]{1,0:T(8,128)S(1)}, f32[320,128]{1,0:T(8,128)S(1)}) custom-call(f32[5,128,128]{2,1,0:T(8,128)S(1)} %get-tuple-element.13.u, f32[160,128]{1,0:T(8,128)S(1)} %get-tuple-element.14.xlo, f32[160,128]{1,0:T(8,128)S(1)} %get-tuple-element.15.xhi, ...), custom_call_target="tpu_custom_call" | custom-call | tf_op jit(solution)/shard_map/middle/pallas_call | solution.py:380
  29.9 1.9 %collective-permute-start.4 = (f32[320,128]{1,0:T(8,128)S(1)}, f32[320,128]{1,0:T(8,128)S(1)}, u32[]{:S(2)}, u32[]{:S(2)}) collective-permute-start(f32[320,128]{1,0:T(8,128)S(1)} %get-tuple-element.21), channel_id=1, source_target_pairs={{0,8},{8,16},{16,24},{24,32},{32,40},{40,48},{48,56},{56,64},{64,7... | collective-permute-start | bytes 491528 | tf_op jit(solution)/shard_map/ppermute | solution.py:348
  31.8 6.7 %collective-permute-start.5 = (f32[320,128]{1,0:T(8,128)S(1)}, f32[320,128]{1,0:T(8,128)S(1)}, u32[]{:S(2)}, u32[]{:S(2)}) collective-permute-start(f32[320,128]{1,0:T(8,128)S(1)} %get-tuple-element.22), channel_id=1, source_target_pairs={{0,760},{8,0},{16,8},{24,16},{32,24},{40,32},{48,40},{56,48},{64,5... | collective-permute-start | bytes 491528 | tf_op jit(solution)/shard_map/ppermute | solution.py:348
  38.5 13.7 %all_to_all.10.peaks = f32[24,1,128]{2,1,0:T(1,128)S(1)} all-to-all(f32[24,1,128]{2,1,0:T(1,128)S(1)} %get-tuple-element.23), channel_id=1, replica_groups={{0,1,64,65,128,129,192,193,256,257,320,321,384,385,448,449,512,513,576,..., dimensions={0} | all-to-all | bytes 24576 | tf_op jit(solution)/shard_map/all_to_all | solution.py:352
  52.2 0.6 merge.1
  52.8 6.0 %all-to-all-start.1 = ((f32[32,1,128]{2,1,0:T(1,128)}), f32[32,1,128]{2,1,0:T(1,128)S(1)}, u32[]{:S(2)}, u32[]{:S(2)}) async-start(f32[32,1,128]{2,1,0:T(1,128)} %merge.1), calls=%async_computation.1 | async-start | bytes 32768 | tf_op jit(solution)/shard_map/all_to_all | solution.py:352
  59.5 7.9 %all-to-all-done.1.peaks = f32[32,1,128]{2,1,0:T(1,128)S(1)} async-done(((f32[32,1,128]{2,1,0:T(1,128)}), f32[32,1,128]{2,1,0:T(1,128)S(1)}, u32[]{:S(2)}, u32[]{:S(2)}) %all-to-all-start.1) | async-done | bytes 16416 | tf_op jit(solution)/shard_map/all_to_all | solution.py:352
  67.4 0.0 collective-permute-done.4.from_left
  67.4 0.0 collective-permute-done.5.from_right
  67.4 1.4 %last.1 = (f32[5,125,1,128]{3,2,1,0:T(1,128)}, f32[5,25,1,128]{3,2,1,0:T(1,128)}) custom-call(s32[1,1]{1,0:T(1,128)S(6)} %copy.7.shifts, f32[5,128,128]{2,1,0:T(8,128)S(1)} %get-tuple-element.13.u, f32[5,128,128]{2,1,0:T(8,128)S(1)} %get-tuple-element.19.a, f32[5,128,128]{2,1,0:T(8,128)S(1)} %get-tuple-element.20.b, ...), custom_call_target="tpu_custom_call" | custom-call | tf_op jit(solution)/shard_map/last/pallas_call | solution.py:412
Async XLA Ops:
  2.1 25.9 %collective-permute-start.2 = (f32[320,128]{1,0:T(8,128)S(1)}, f32[320,128]{1,0:T(8,128)S(1)}, u32[]{:S(2)}, u32[]{:S(2)}) collective-permute-start(f32[320,128]{1,0:T(8,128)S(1)} %get-tuple-element.16.up), channel_id=1, source_target_pairs={{0,8},{8,16},{16,24},{24,32},{32,40},{40,48},{48,56},{56,64},{64,7... | collective-permute-start | bytes 491528 | tf_op jit(solution)/shard_map/ppermute | solution.py:348
  6.1 21.9 %collective-permute-start.3 = (f32[320,128]{1,0:T(8,128)S(1)}, f32[320,128]{1,0:T(8,128)S(1)}, u32[]{:S(2)}, u32[]{:S(2)}) collective-permute-start(f32[320,128]{1,0:T(8,128)S(1)} %get-tuple-element.17.down), channel_id=1, source_target_pairs={{0,760},{8,0},{16,8},{24,16},{32,24},{40,32},{48,40},{56,48},{64,5... | collective-permute-start | bytes 491528 | tf_op jit(solution)/shard_map/ppermute | solution.py:348
  22.0 3.5 %collective-permute-start = (f32[160,128]{1,0:T(8,128)S(1)}, f32[160,128]{1,0:T(8,128)S(1)}, u32[]{:S(2)}, u32[]{:S(2)}) collective-permute-start(f32[160,128]{1,0:T(8,128)S(1)} %get-tuple-element.15.xhi), channel_id=1, source_target_pairs={{0,1},{1,2},{2,3},{3,4},{4,5},{5,6},{6,7},{7,0},{8,9},{9,10},{10,1... | collective-permute-start | bytes 245768 | tf_op jit(solution)/shard_map/ppermute | solution.py:348
  24.1 3.9 %collective-permute-start.1 = (f32[160,128]{1,0:T(8,128)S(1)}, f32[160,128]{1,0:T(8,128)S(1)}, u32[]{:S(2)}, u32[]{:S(2)}) collective-permute-start(f32[160,128]{1,0:T(8,128)S(1)} %get-tuple-element.14.xlo), channel_id=1, source_target_pairs={{0,7},{1,0},{2,1},{3,2},{4,3},{5,4},{6,5},{7,6},{8,15},{9,8},{10,9... | collective-permute-start | bytes 245768 | tf_op jit(solution)/shard_map/ppermute | solution.py:348
  29.9 37.5 %collective-permute-start.4 = (f32[320,128]{1,0:T(8,128)S(1)}, f32[320,128]{1,0:T(8,128)S(1)}, u32[]{:S(2)}, u32[]{:S(2)}) collective-permute-start(f32[320,128]{1,0:T(8,128)S(1)} %get-tuple-element.21), channel_id=1, source_target_pairs={{0,8},{8,16},{16,24},{24,32},{32,40},{40,48},{48,56},{56,64},{64,7... | collective-permute-start | bytes 491528 | tf_op jit(solution)/shard_map/ppermute | solution.py:348
  31.8 35.5 %collective-permute-start.5 = (f32[320,128]{1,0:T(8,128)S(1)}, f32[320,128]{1,0:T(8,128)S(1)}, u32[]{:S(2)}, u32[]{:S(2)}) collective-permute-start(f32[320,128]{1,0:T(8,128)S(1)} %get-tuple-element.22), channel_id=1, source_target_pairs={{0,760},{8,0},{16,8},{24,16},{32,24},{40,32},{48,40},{56,48},{64,5... | collective-permute-start | bytes 491528 | tf_op jit(solution)/shard_map/ppermute | solution.py:348
  52.8 14.6 %all-to-all-start.1 = ((f32[32,1,128]{2,1,0:T(1,128)}), f32[32,1,128]{2,1,0:T(1,128)S(1)}, u32[]{:S(2)}, u32[]{:S(2)}) async-start(f32[32,1,128]{2,1,0:T(1,128)} %merge.1), calls=%async_computation.1 | async-start | bytes 32768 | tf_op jit(solution)/shard_map/all_to_all | solution.py:352

commit v5 on v4

--- a/solution.py
+++ b/solution.py
@@ -29,13 +29,13 @@
 
 def plane_groups():
     return [
-        [flat(z, y, x, c) for y in range(Y) for x in range(X)] for z in range(Z) for c in range(CORES)
+        [flat(z, (y + 6) % Y, (x + 0) % X, c) for y in range(Y) for x in range(X)] for z in range(Z) for c in range(CORES)
     ]
 
 
 def column_groups():
     return [
-        [flat(z, y, x, c) for z in range(Z) for c in range(CORES)] for y in range(Y) for x in range(X)
+        [flat((z + 11) % Z, y, x, c) for z in range(Z) for c in range(CORES)] for y in range(Y) for x in range(X)
     ]
 
 
@@ -147,6 +147,10 @@
         at = slice(base + row, base + row + 1)
         inside = (lane[:1] >= LANES * g) & (lane[:1] < LANES * (g + 1))
         out[at, :] = jnp.where(inside, line, out[at, :])
+
+
+def first_up():
+    return lax.axis_index("curve") % 2 == 1
 
 
 def start_kernel(state, levels, u, scale_row, peak, xlo, xhi, down, up, level, best, sem):
@@ -206,7 +210,7 @@
 
 def middle_kernel(
     u, xlo, xhi, xbelow, xabove, up, down, below, above, neighbours, scale_row, operator,
-    a_out, b_out, to_left, to_right, ylo, yhi, rhs_top, rhs_rest, out_top, out_rest, named, table, sem,
+    a_out, b_out, to_near, to_far, to_left, to_right, ylo, yhi, rhs_top, rhs_rest, out_top, out_rest, named, table, sem,
 ):
     fetches = [
         pltpu.make_async_copy(neighbours, named, sem.at[0]),
@@ -264,6 +268,8 @@
         packed(ref, to_left, i * PACK, 0)
         packed(ref, to_right, i * PACK, EL - LANES)
         spread(ref, to_right, i * PACK)
+    to_near[...] = jnp.where(first_up(), to_right[...], to_left[...])
+    to_far[...] = jnp.where(first_up(), to_left[...], to_right[...])
 
 
 def merge_kernel(peaks, peak):
@@ -272,7 +278,7 @@
 
 
 def last_kernel(
-    shifts, u, a, b, below, above, from_left, from_right, peaks, moved, mortar, new, surface, halos, sem
+    shifts, u, a, b, below, above, from_near, from_far, peaks, moved, mortar, new, surface, halos, sem
 ):
     best = jnp.max(peaks[...], axis=0)
     lam = jnp.max(best[:, : EL // 2], axis=1, keepdims=True)
@@ -291,8 +297,9 @@
     far = lane_up < jnp.where(shift == -SHIFT_MAX, 1, 0)
     trace = slice(NV * FPAD, NV * FPAD + PACK)
     pack = jnp.where(ahead, above[trace, :], below[trace, :])
-    rate = jnp.where(ahead, from_right[:PACK], from_left[:PACK]) + lam * jnp.where(
-        ahead, from_right[PACK:], from_left[PACK:]
+    nearer = jnp.logical_not(jnp.logical_xor(ahead, first_up()))
+    rate = jnp.where(nearer, from_near[:PACK], from_far[:PACK]) + lam * jnp.where(
+        nearer, from_near[PACK:], from_far[PACK:]
     )
     pack = pack + step * rate
     back = jnp.where(ahead, 0, LANES) + shift
@@ -346,6 +353,12 @@
 def shifted(value, axis, step):
     count = lax.axis_size(axis)
     return lax.ppermute(value, axis, [(i, (i + step) % count) for i in range(count)])
+
+
+def swapped(value, start):
+    count = lax.axis_size("curve")
+    pairs = [(start + k, (start + k + 1) % count) for k in range(0, count, 2)]
+    return lax.ppermute(value, "curve", pairs + [(b, a) for a, b in pairs])
 
 
 def exchanged(value, groups):
@@ -377,12 +390,14 @@
     xabove = shifted(xlo, "slab", -1)
     below = shifted(up, "curve", 1)
     above = shifted(down, "curve", -1)
-    a, b, to_left, to_right = pl.pallas_call(
+    a, b, to_near, to_far = pl.pallas_call(
         middle_kernel,
         out_shape=(block, block, halo, halo),
         in_specs=[VMEM] * 9 + [HBM, VMEM, HBM],
         out_specs=(VMEM,) * 4,
         scratch_shapes=[
+            pltpu.VMEM(halo.shape, jnp.float32),
+            pltpu.VMEM(halo.shape, jnp.float32),
             pltpu.VMEM((NV * FPAD, EL), jnp.float32),
             pltpu.VMEM((NV * FPAD, EL), jnp.float32),
             pltpu.VMEM((3 * PAD + 6 * FPAD, NV * EL), jnp.bfloat16),
@@ -407,8 +422,8 @@
         name="merge",
     )(peak)
     peak = exchanged(peak, columns)
-    from_left = shifted(to_right, "curve", 1)
-    from_right = shifted(to_left, "curve", -1)
+    from_near = swapped(to_near, 1)
+    from_far = swapped(to_far, 0)
     return pl.pallas_call(
         last_kernel,
         out_shape=(shape(NV, NODES, 1, EL), shape(NV, FACE, 1, EL)),
@@ -422,7 +437,7 @@
         ],
         compiler_params=pltpu.CompilerParams(vmem_limit_bytes=8 << 20),
         name="last",
-    )(shifts, u, a, b, below, above, from_left, from_right, peak)
+    )(shifts, u, a, b, below, above, from_near, from_far, peak)
 
 
 def solution(mesh):

time: 69.1 us -> 66.6 us (0.964)
  waiting for transfers between devices: 11.8 us -> 8.8 us
    ppermute x6 -> x4, starting transfers between devices: 30.6 us -> 22 us  [shifted(): lax.ppermute(value, axis, [(i, (i + step) % count) for i in range(count)])]
    ppermute x0 -> x2, starting transfers between devices: none -> 6.27 us  [swapped(): return lax.ppermute(value, 'curve', pairs + [(b, a) for a, b in pairs])]
    all_to_all x1, waiting for transfers between devices: 7.89 us -> 4.93 us  [exchanged(): lax.all_to_all(value, AXES, 0, 0, tiled=True, axis_index_groups=groups)]
    all_to_all x1, starting transfers between devices: 6.02 us -> 8.92 us  [exchanged(): lax.all_to_all(value, AXES, 0, 0, tiled=True, axis_index_groups=groups)]
    ppermute x6 -> x4, waiting for transfers between devices: 3.87 us -> 3.87 us  [shifted(): lax.ppermute(value, axis, [(i, (i + step) % count) for i in range(count)])]
where the time goes in v5:
time: 66.6 us; the launch traced here: 66.2 us
  starting transfers between devices  37.2 us (56%)
  blocking collectives  13.5 us (20%)
  waiting for transfers between devices  8.8 us (13%)
  Pallas kernels  5.37 us (8%)
  between operations  1.34 us (2%)
    ppermute x4, starting transfers between devices, shifted(): lax.ppermute(value, axis, [(i, (i + step) % count) for i in range(count)])  22 us
    all_to_all x1, blocking collectives, exchanged(): lax.all_to_all(value, AXES, 0, 0, tiled=True, axis_index_groups=groups)  13.5 us
    all_to_all x1, starting transfers between devices, exchanged(): lax.all_to_all(value, AXES, 0, 0, tiled=True, axis_index_groups=groups)  8.92 us
    ppermute x2, starting transfers between devices, swapped(): return lax.ppermute(value, 'curve', pairs + [(b, a) for a, b in pairs])  6.27 us
    all_to_all x1, waiting for transfers between devices, exchanged(): lax.all_to_all(value, AXES, 0, 0, tiled=True, axis_index_groups=groups)  4.93 us
    ppermute x4, waiting for transfers between devices, shifted(): lax.ppermute(value, axis, [(i, (i + step) % count) for i in range(count)])  3.87 us
    pallas_call x1, Pallas kernels, substep(): pl.pallas_call(middle_kernel, out_shape=(block, block, halo, halo), in_sp...  1.92 us
    pallas_call x1, Pallas kernels, substep(): pl.pallas_call(start_kernel, out_shape=(block, shape(1, EL), shape(len(pl...  1.44 us
  transfers between devices with their start and end apart: 7, of which 3 were waited for; matrix products, arithmetic and copies ran while one was open for 0% of the time, Pallas kernels for 1%

profile of v5, /device:TPU:1, one launch (start us, length us, event | category | flops | bytes accessed | tf_op | source)
XLA Modules:
  0.0 66.2 jit_solution(8876155116510397101)
XLA Ops:
  0.6 1.4 %start.1 = (f32[5,128,128]{2,1,0:T(8,128)S(1)}, f32[1,128]{1,0:T(1,128)S(1)}, f32[24,1,128]{2,1,0:T(1,128)S(1)}, f32[160,128]{1,0:T(8,128)S(1)}, f32[160,128]{1,...) custom-call(f32[5,125,1,128]{3,2,1,0:T(1,128)} %state.1, s32[1,128]{1,0:T(1,128)} %levels.1), custom_call_target="tpu_custom_call" | custom-call | tf_op jit(solution)/shard_map/start/pallas_call | solution.py:375
  2.1 4.0 %collective-permute-start.2 = (f32[320,128]{1,0:T(8,128)S(1)}, f32[320,128]{1,0:T(8,128)S(1)}, u32[]{:S(2)}, u32[]{:S(2)}) collective-permute-start(f32[320,128]{1,0:T(8,128)S(1)} %get-tuple-element.16.up), channel_id=1, source_target_pairs={{0,8},{8,16},{16,24},{24,32},{32,40},{40,48},{48,56},{56,64},{64,7... | collective-permute-start | bytes 491528 | tf_op jit(solution)/shard_map/ppermute | solution.py:355
  6.1 15.9 %collective-permute-start.3 = (f32[320,128]{1,0:T(8,128)S(1)}, f32[320,128]{1,0:T(8,128)S(1)}, u32[]{:S(2)}, u32[]{:S(2)}) collective-permute-start(f32[320,128]{1,0:T(8,128)S(1)} %get-tuple-element.17.down), channel_id=1, source_target_pairs={{0,760},{8,0},{16,8},{24,16},{32,24},{40,32},{48,40},{56,48},{64,5... | collective-permute-start | bytes 491528 | tf_op jit(solution)/shard_map/ppermute | solution.py:355
  22.0 2.1 %collective-permute-start = (f32[160,128]{1,0:T(8,128)S(1)}, f32[160,128]{1,0:T(8,128)S(1)}, u32[]{:S(2)}, u32[]{:S(2)}) collective-permute-start(f32[160,128]{1,0:T(8,128)S(1)} %get-tuple-element.15.xhi), channel_id=1, source_target_pairs={{0,1},{1,2},{2,3},{3,4},{4,5},{5,6},{6,7},{7,0},{8,9},{9,10},{10,1... | collective-permute-start | bytes 245768 | tf_op jit(solution)/shard_map/ppermute | solution.py:355
  24.1 0.0 collective-permute-start.1
  24.1 1.5 %collective-permute-done.xbelow = f32[160,128]{1,0:T(8,128)S(1)} collective-permute-done((f32[160,128]{1,0:T(8,128)S(1)}, f32[160,128]{1,0:T(8,128)S(1)}, u32[]{:S(2)}, u32[]{:S(2)}) %collective-permute-start) | collective-permute-done | bytes 81952 | tf_op jit(solution)/shard_map/ppermute | solution.py:355
  25.6 2.4 %collective-permute-done.1.xabove = f32[160,128]{1,0:T(8,128)S(1)} collective-permute-done((f32[160,128]{1,0:T(8,128)S(1)}, f32[160,128]{1,0:T(8,128)S(1)}, u32[]{:S(2)}, u32[]{:S(2)}) %collective-permute-start.1) | collective-permute-done | bytes 81952 | tf_op jit(solution)/shard_map/ppermute | solution.py:355
  28.0 0.0 collective-permute-done.2.below
  28.0 0.0 collective-permute-done.3.above
  28.0 1.9 %middle.1 = (f32[5,128,128]{2,1,0:T(8,128)S(1)}, f32[5,128,128]{2,1,0:T(8,128)S(1)}, f32[320,128]{1,0:T(8,128)S(1)}, f32[320,128]{1,0:T(8,128)S(1)}) custom-call(f32[5,128,128]{2,1,0:T(8,128)S(1)} %get-tuple-element.13.u, f32[160,128]{1,0:T(8,128)S(1)} %get-tuple-element.14.xlo, f32[160,128]{1,0:T(8,128)S(1)} %get-tuple-element.15.xhi, ...), custom_call_target="tpu_custom_call" | custom-call | tf_op jit(solution)/shard_map/middle/pallas_call | solution.py:393
  29.9 4.4 %collective-permute-start.4 = (f32[320,128]{1,0:T(8,128)S(1)}, f32[320,128]{1,0:T(8,128)S(1)}, u32[]{:S(2)}, u32[]{:S(2)}) collective-permute-start(f32[320,128]{1,0:T(8,128)S(1)} %get-tuple-element.21), channel_id=1, source_target_pairs={{8,16},{24,32},{40,48},{56,64},{72,80},{88,96},{104,112},{120,128}... | collective-permute-start | bytes 491528 | tf_op jit(solution)/shard_map/ppermute | solution.py:361
  34.3 1.9 %collective-permute-start.5 = (f32[320,128]{1,0:T(8,128)S(1)}, f32[320,128]{1,0:T(8,128)S(1)}, u32[]{:S(2)}, u32[]{:S(2)}) collective-permute-start(f32[320,128]{1,0:T(8,128)S(1)} %get-tuple-element.22), channel_id=1, source_target_pairs={{0,8},{16,24},{32,40},{48,56},{64,72},{80,88},{96,104},{112,120},{... | collective-permute-start | bytes 491528 | tf_op jit(solution)/shard_map/ppermute | solution.py:361
  36.2 13.5 %all_to_all.10.peaks = f32[24,1,128]{2,1,0:T(1,128)S(1)} all-to-all(f32[24,1,128]{2,1,0:T(1,128)S(1)} %get-tuple-element.23), channel_id=1, replica_groups={{704,705,0,1,64,65,128,129,192,193,256,257,320,321,384,385,448,449,512,..., dimensions={0} | all-to-all | bytes 24576 | tf_op jit(solution)/shard_map/all_to_all | solution.py:365
  49.7 0.6 merge.1
  50.3 8.9 %all-to-all-start.1 = ((f32[32,1,128]{2,1,0:T(1,128)}), f32[32,1,128]{2,1,0:T(1,128)S(1)}, u32[]{:S(2)}, u32[]{:S(2)}) async-start(f32[32,1,128]{2,1,0:T(1,128)} %merge.1), calls=%async_computation.1 | async-start | bytes 32768 | tf_op jit(solution)/shard_map/all_to_all | solution.py:365
  59.9 4.9 %all-to-all-done.1.peaks = f32[32,1,128]{2,1,0:T(1,128)S(1)} async-done(((f32[32,1,128]{2,1,0:T(1,128)}), f32[32,1,128]{2,1,0:T(1,128)S(1)}, u32[]{:S(2)}, u32[]{:S(2)}) %all-to-all-start.1) | async-done | bytes 16416 | tf_op jit(solution)/shard_map/all_to_all | solution.py:365
  64.8 0.0 collective-permute-done.4.from_near
  64.8 0.0 collective-permute-done.5.from_far
  64.8 1.4 %last.1 = (f32[5,125,1,128]{3,2,1,0:T(1,128)}, f32[5,25,1,128]{3,2,1,0:T(1,128)}) custom-call(s32[1,1]{1,0:T(1,128)S(6)} %copy.7.shifts, f32[5,128,128]{2,1,0:T(8,128)S(1)} %get-tuple-element.13.u, f32[5,128,128]{2,1,0:T(8,128)S(1)} %get-tuple-element.19.a, f32[5,128,128]{2,1,0:T(8,128)S(1)} %get-tuple-element.20.b, ...), custom_call_target="tpu_custom_call" | custom-call | tf_op jit(solution)/shard_map/last/pallas_call | solution.py:427
Async XLA Ops:
  2.1 25.9 %collective-permute-start.2 = (f32[320,128]{1,0:T(8,128)S(1)}, f32[320,128]{1,0:T(8,128)S(1)}, u32[]{:S(2)}, u32[]{:S(2)}) collective-permute-start(f32[320,128]{1,0:T(8,128)S(1)} %get-tuple-element.16.up), channel_id=1, source_target_pairs={{0,8},{8,16},{16,24},{24,32},{32,40},{40,48},{48,56},{56,64},{64,7... | collective-permute-start | bytes 491528 | tf_op jit(solution)/shard_map/ppermute | solution.py:355
  6.1 21.9 %collective-permute-start.3 = (f32[320,128]{1,0:T(8,128)S(1)}, f32[320,128]{1,0:T(8,128)S(1)}, u32[]{:S(2)}, u32[]{:S(2)}) collective-permute-start(f32[320,128]{1,0:T(8,128)S(1)} %get-tuple-element.17.down), channel_id=1, source_target_pairs={{0,760},{8,0},{16,8},{24,16},{32,24},{40,32},{48,40},{56,48},{64,5... | collective-permute-start | bytes 491528 | tf_op jit(solution)/shard_map/ppermute | solution.py:355
  22.0 3.5 %collective-permute-start = (f32[160,128]{1,0:T(8,128)S(1)}, f32[160,128]{1,0:T(8,128)S(1)}, u32[]{:S(2)}, u32[]{:S(2)}) collective-permute-start(f32[160,128]{1,0:T(8,128)S(1)} %get-tuple-element.15.xhi), channel_id=1, source_target_pairs={{0,1},{1,2},{2,3},{3,4},{4,5},{5,6},{6,7},{7,0},{8,9},{9,10},{10,1... | collective-permute-start | bytes 245768 | tf_op jit(solution)/shard_map/ppermute | solution.py:355
  24.1 3.9 %collective-permute-start.1 = (f32[160,128]{1,0:T(8,128)S(1)}, f32[160,128]{1,0:T(8,128)S(1)}, u32[]{:S(2)}, u32[]{:S(2)}) collective-permute-start(f32[160,128]{1,0:T(8,128)S(1)} %get-tuple-element.14.xlo), channel_id=1, source_target_pairs={{0,7},{1,0},{2,1},{3,2},{4,3},{5,4},{6,5},{7,6},{8,15},{9,8},{10,9... | collective-permute-start | bytes 245768 | tf_op jit(solution)/shard_map/ppermute | solution.py:355
  29.9 34.9 %collective-permute-start.4 = (f32[320,128]{1,0:T(8,128)S(1)}, f32[320,128]{1,0:T(8,128)S(1)}, u32[]{:S(2)}, u32[]{:S(2)}) collective-permute-start(f32[320,128]{1,0:T(8,128)S(1)} %get-tuple-element.21), channel_id=1, source_target_pairs={{8,16},{24,32},{40,48},{56,64},{72,80},{88,96},{104,112},{120,128}... | collective-permute-start | bytes 491528 | tf_op jit(solution)/shard_map/ppermute | solution.py:361
  34.3 30.6 %collective-permute-start.5 = (f32[320,128]{1,0:T(8,128)S(1)}, f32[320,128]{1,0:T(8,128)S(1)}, u32[]{:S(2)}, u32[]{:S(2)}) collective-permute-start(f32[320,128]{1,0:T(8,128)S(1)} %get-tuple-element.22), channel_id=1, source_target_pairs={{0,8},{16,24},{32,40},{48,56},{64,72},{80,88},{96,104},{112,120},{... | collective-permute-start | bytes 491528 | tf_op jit(solution)/shard_map/ppermute | solution.py:361
  50.3 14.5 %all-to-all-start.1 = ((f32[32,1,128]{2,1,0:T(1,128)}), f32[32,1,128]{2,1,0:T(1,128)S(1)}, u32[]{:S(2)}, u32[]{:S(2)}) async-start(f32[32,1,128]{2,1,0:T(1,128)} %merge.1), calls=%async_computation.1 | async-start | bytes 32768 | tf_op jit(solution)/shard_map/all_to_all | solution.py:365

commit v6 on v5

--- a/solution.py
+++ b/solution.py
@@ -153,12 +153,19 @@
     return lax.axis_index("curve") % 2 == 1
 
 
-def start_kernel(state, levels, u, scale_row, peak, xlo, xhi, down, up, level, best, sem):
+def start_kernel(
+    state, levels, neighbours, operator,
+    u, scale_row, peak, xlo, xhi, down, up, named, table, level, best, sem,
+):
     copies = [
         pltpu.make_async_copy(state.at[v, :, 0], u.at[v, pl.ds(0, NODES)], sem.at[v]) for v in range(NV)
     ]
     copies.append(pltpu.make_async_copy(levels, level, sem.at[NV]))
-    for copy in copies:
+    sends = [
+        pltpu.make_async_copy(neighbours, named, sem.at[NV + 2]),
+        pltpu.make_async_copy(operator, table, sem.at[NV + 3]),
+    ]
+    for copy in copies + sends:
         copy.start()
     for v in range(NV):
         u[v, NODES:PAD, :] = jnp.full((PAD - NODES, EL), 1.0 if v == 0 else 0.0, jnp.float32)
@@ -178,8 +185,8 @@
     lam = jnp.max(speed, axis=1, keepdims=True)
     top = jnp.max(speed * scale, axis=1, keepdims=True)
     best[...] = jnp.broadcast_to(lane_pair(lam, top)[None], best.shape)
-    send = pltpu.make_async_copy(best, peak, sem.at[NV + 1])
-    send.start()
+    sends.append(pltpu.make_async_copy(best, peak, sem.at[NV + 1]))
+    sends[-1].start()
     ones = jnp.full((FPAD - FACE, EL), 1.0, jnp.float32)
     for v in range(NV):
         row = v * FPAD
@@ -192,7 +199,8 @@
     packed(u, down, NV * FPAD, 0)
     packed(u, up, NV * FPAD, EL - LANES)
     spread(u, up, NV * FPAD)
-    send.wait()
+    for send in sends:
+        send.wait()
 
 
 def dot(a, b):
@@ -209,15 +217,9 @@
 
 
 def middle_kernel(
-    u, xlo, xhi, xbelow, xabove, up, down, below, above, neighbours, scale_row, operator,
-    a_out, b_out, to_near, to_far, to_left, to_right, ylo, yhi, rhs_top, rhs_rest, out_top, out_rest, named, table, sem,
+    u, xlo, xhi, xbelow, xabove, up, down, below, above, named, scale_row, volume, table,
+    a_out, b_out, to_near, to_far, to_left, to_right, ylo, yhi, rhs_top, rhs_rest, out_top, out_rest,
 ):
-    fetches = [
-        pltpu.make_async_copy(neighbours, named, sem.at[0]),
-        pltpu.make_async_copy(operator, table, sem.at[1]),
-    ]
-    for fetch in fetches:
-        fetch.start()
     scale = scale_row[...]
     ones = jnp.full((FPAD - FACE, EL), 1.0, jnp.float32)
     for v in range(NV):
@@ -227,12 +229,6 @@
             yhi[row + 5 * k : row + 5 * k + 5, :] = u[v, 25 * k + 20 : 25 * k + 25, :]
         ylo[row + FACE : row + FPAD, :] = ones
         yhi[row + FACE : row + FPAD, :] = ones
-
-    for d, parts in enumerate(all_fluxes([u[v] for v in range(NV)])):
-        for v in range(NV):
-            at = (slice(d * PAD, (d + 1) * PAD), slice(v * EL, (v + 1) * EL))
-            rhs_top[at], rhs_rest[at] = halves(parts[v])
-    fetches[0].wait()
     home = named[2] >> 7
     half = 0.5 / END_WEIGHT
     nodes = NV * FPAD
@@ -252,15 +248,12 @@
         rows = slice(f * FPAD, (f + 1) * FPAD)
         for v in range(NV):
             lanes = slice(v * EL, (v + 1) * EL)
-            at = (slice(3 * PAD + f * FPAD, 3 * PAD + (f + 1) * FPAD), lanes)
-            rhs_top[at], rhs_rest[at] = halves(sign * parts[v])
+            rhs_top[rows, lanes], rhs_rest[rows, lanes] = halves(sign * parts[v])
             jump = half * (values[v] - own[v * FPAD : (v + 1) * FPAD, :])
             out_top[rows, lanes], out_rest[rows, lanes] = halves(jump)
-    fetches[1].wait()
-    first = dot(table[...][:, : 3 * PAD], rhs_top[: 3 * PAD, :])
-    a = first[:PAD] + first[PAD:] + dot(table[:PAD, :], rhs_rest[...])
-    a = a + dot(table[:PAD, 3 * PAD :], rhs_top[3 * PAD :, :])
-    b = dot(table[:PAD, 3 * PAD :], out_top[...]) + dot(table[:PAD, 3 * PAD :], out_rest[...])
+    place = table[:PAD, 3 * PAD :]
+    a = volume[...] + (dot(place, rhs_top[...]) + dot(place, rhs_rest[...]))
+    b = dot(place, out_top[...]) + dot(place, out_rest[...])
     for v in range(NV):
         a_out[v] = a[:, v * EL : (v + 1) * EL] * scale
         b_out[v] = b[:, v * EL : (v + 1) * EL] * scale
@@ -272,9 +265,18 @@
     to_far[...] = jnp.where(first_up(), to_left[...], to_right[...])
 
 
-def merge_kernel(peaks, peak):
+def merge_kernel(peaks, u, table, peak, volume, wide, rhs_top, rhs_rest, sem):
     best = jnp.max(peaks[...], axis=0)
-    peak[...] = jnp.broadcast_to(best[None], peak.shape)
+    wide[...] = jnp.broadcast_to(best[None], wide.shape)
+    send = pltpu.make_async_copy(wide, peak, sem)
+    send.start()
+    for d, parts in enumerate(all_fluxes([u[v] for v in range(NV)])):
+        for v in range(NV):
+            at = (slice(d * PAD, (d + 1) * PAD), slice(v * EL, (v + 1) * EL))
+            rhs_top[at], rhs_rest[at] = halves(parts[v])
+    both = dot(table[:, : 3 * PAD], rhs_top[...])
+    volume[...] = both[:PAD] + (both[PAD:] + dot(table[:PAD, : 3 * PAD], rhs_rest[...]))
+    send.wait()
 
 
 def last_kernel(
@@ -372,55 +374,60 @@
     edge = shape(NV * FPAD + PACK, EL)
     halo = shape(2 * PACK, EL)
     block = shape(NV, PAD, EL)
-    u, scale, peak, xlo, xhi, down, up = pl.pallas_call(
+    u, scale, peak, xlo, xhi, down, up, named, table = pl.pallas_call(
         start_kernel,
-        out_shape=(block, shape(1, EL), shape(len(planes[0]), 1, EL), trace, trace, edge, edge),
-        in_specs=[HBM, HBM],
-        out_specs=(VMEM, VMEM, HBM) + (VMEM,) * 4,
+        out_shape=(block, shape(1, EL), shape(len(planes[0]), 1, EL), trace, trace, edge, edge)
+        + (jax.ShapeDtypeStruct(neighbours.shape, jnp.int32),)
+        + (jax.ShapeDtypeStruct(operator.shape, jnp.bfloat16),),
+        in_specs=[HBM] * 4,
+        out_specs=(VMEM, VMEM, HBM) + (VMEM,) * 6,
         scratch_shapes=[
             pltpu.VMEM((1, EL), jnp.int32),
             pltpu.VMEM((len(planes[0]), 1, EL), jnp.float32),
-            pltpu.SemaphoreType.DMA((NV + 2,)),
+            pltpu.SemaphoreType.DMA((NV + 4,)),
         ],
-        compiler_params=pltpu.CompilerParams(vmem_limit_bytes=4 << 20),
+        compiler_params=pltpu.CompilerParams(vmem_limit_bytes=8 << 20),
         name="start",
-    )(held(state), held(levels))
+    )(held(state), held(levels), held(neighbours), held(operator))
     peak = exchanged(peak, planes)
     xbelow = shifted(xhi, "slab", 1)
     xabove = shifted(xlo, "slab", -1)
     below = shifted(up, "curve", 1)
     above = shifted(down, "curve", -1)
+    peak, volume = pl.pallas_call(
+        merge_kernel,
+        out_shape=(shape(len(columns[0]), 1, EL), shape(PAD, NV * EL)),
+        in_specs=[VMEM] * 3,
+        out_specs=(HBM, VMEM),
+        scratch_shapes=[
+            pltpu.VMEM((len(columns[0]), 1, EL), jnp.float32),
+            pltpu.VMEM((3 * PAD, NV * EL), jnp.bfloat16),
+            pltpu.VMEM((3 * PAD, NV * EL), jnp.bfloat16),
+            pltpu.SemaphoreType.DMA(()),
+        ],
+        compiler_params=pltpu.CompilerParams(vmem_limit_bytes=6 << 20),
+        name="merge",
+    )(peak, u, table)
     a, b, to_near, to_far = pl.pallas_call(
         middle_kernel,
         out_shape=(block, block, halo, halo),
-        in_specs=[VMEM] * 9 + [HBM, VMEM, HBM],
+        in_specs=[VMEM] * 13,
         out_specs=(VMEM,) * 4,
         scratch_shapes=[
             pltpu.VMEM(halo.shape, jnp.float32),
             pltpu.VMEM(halo.shape, jnp.float32),
             pltpu.VMEM((NV * FPAD, EL), jnp.float32),
             pltpu.VMEM((NV * FPAD, EL), jnp.float32),
-            pltpu.VMEM((3 * PAD + 6 * FPAD, NV * EL), jnp.bfloat16),
-            pltpu.VMEM((3 * PAD + 6 * FPAD, NV * EL), jnp.bfloat16),
             pltpu.VMEM((6 * FPAD, NV * EL), jnp.bfloat16),
             pltpu.VMEM((6 * FPAD, NV * EL), jnp.bfloat16),
-            pltpu.VMEM((6, 1, EL), jnp.int32),
-            pltpu.VMEM(operator.shape, jnp.bfloat16),
-            pltpu.SemaphoreType.DMA((2,)),
+            pltpu.VMEM((6 * FPAD, NV * EL), jnp.bfloat16),
+            pltpu.VMEM((6 * FPAD, NV * EL), jnp.bfloat16),
         ],
         compiler_params=pltpu.CompilerParams(vmem_limit_bytes=12 << 20),
         name="middle",
     )(
-        u, xlo, xhi, xbelow, xabove, up, down, below, above, held(neighbours), scale, held(operator)
+        u, xlo, xhi, xbelow, xabove, up, down, below, above, named, scale, volume, table
     )
-    peak = pl.pallas_call(
-        merge_kernel,
-        out_shape=shape(len(columns[0]), 1, EL),
-        in_specs=[VMEM],
-        out_specs=VMEM,
-        compiler_params=pltpu.CompilerParams(vmem_limit_bytes=1 << 20),
-        name="merge",
-    )(peak)
     peak = exchanged(peak, columns)
     from_near = swapped(to_near, 1)
     from_far = swapped(to_far, 0)

time: 66.6 us -> 62.2 us (0.934)
  waiting for transfers between devices: 8.8 us -> 4.94 us
    ppermute x4, waiting for transfers between devices: 3.87 us -> 0.01 us  [shifted(): lax.ppermute(value, axis, [(i, (i + step) % count) for i in range(count)])]
    pallas_call x1, Pallas kernels: 1.92 us -> 0.93 us  [substep(): pl.pallas_call(middle_kernel, out_shape=(block, block, halo, halo), in_sp...]
  transfers between devices with their start and end apart: 7 -> 7, of which waited for: 3 -> 1; matrix products, arithmetic and copies ran while one was open for 0% -> 0% of each run, Pallas kernels for 1% -> 2%
where the time goes in v6:
time: 62.2 us; the launch traced here: 61.5 us
  starting transfers between devices  36.7 us (59%)
  blocking collectives  13.5 us (22%)
  waiting for transfers between devices  4.94 us (8%)
  Pallas kernels  4.88 us (8%)
  between operations  1.37 us (2%)
    ppermute x4, starting transfers between devices, shifted(): lax.ppermute(value, axis, [(i, (i + step) % count) for i in range(count)])  22 us
    all_to_all x1, blocking collectives, exchanged(): lax.all_to_all(value, AXES, 0, 0, tiled=True, axis_index_groups=groups)  13.5 us
    all_to_all x1, starting transfers between devices, exchanged(): lax.all_to_all(value, AXES, 0, 0, tiled=True, axis_index_groups=groups)  8.56 us
    ppermute x2, starting transfers between devices, swapped(): return lax.ppermute(value, 'curve', pairs + [(b, a) for a, b in pairs])  6.17 us
    all_to_all x1, waiting for transfers between devices, exchanged(): lax.all_to_all(value, AXES, 0, 0, tiled=True, axis_index_groups=groups)  4.93 us
    pallas_call x1, Pallas kernels, substep(): pl.pallas_call(start_kernel, out_shape=(block, shape(1, EL), shape(len(pl...  1.46 us
    pallas_call x1, Pallas kernels, substep(): pl.pallas_call(last_kernel, out_shape=(shape(NV, NODES, 1, EL), shape(NV,...  1.39 us
  transfers between devices with their start and end apart: 7, of which 1 were waited for; matrix products, arithmetic and copies ran while one was open for 0% of the time, Pallas kernels for 2%

profile of v6, /device:TPU:1, one launch (start us, length us, event | category | flops | bytes accessed | tf_op | source)
XLA Modules:
  0.0 61.5 jit_solution(9363411406894000858)
XLA Ops:
  0.6 1.5 %start.1 = (f32[5,128,128]{2,1,0:T(8,128)S(1)}, f32[1,128]{1,0:T(1,128)S(1)}, f32[24,1,128]{2,1,0:T(1,128)S(1)}, f32[160,128]{1,0:T(8,128)S(1)}, f32[160,128]{1,...) custom-call(f32[5,125,1,128]{3,2,1,0:T(1,128)} %state.1, ...), custom_call_target="tpu_custom_call" | custom-call | tf_op jit(solution)/shard_map/start/pallas_call | solution.py:377
  2.1 4.0 %collective-permute-start.2 = (f32[320,128]{1,0:T(8,128)S(1)}, f32[320,128]{1,0:T(8,128)S(1)}, u32[]{:S(2)}, u32[]{:S(2)}) collective-permute-start(f32[320,128]{1,0:T(8,128)S(1)} %get-tuple-element.20.up), channel_id=1, source_target_pairs={{0,8},{8,16},{16,24},{24,32},{32,40},{40,48},{48,56},{56,64},{64,7... | collective-permute-start | bytes 491528 | tf_op jit(solution)/shard_map/ppermute | solution.py:357
  6.1 15.9 %collective-permute-start.3 = (f32[320,128]{1,0:T(8,128)S(1)}, f32[320,128]{1,0:T(8,128)S(1)}, u32[]{:S(2)}, u32[]{:S(2)}) collective-permute-start(f32[320,128]{1,0:T(8,128)S(1)} %get-tuple-element.21.down), channel_id=1, source_target_pairs={{0,760},{8,0},{16,8},{24,16},{32,24},{40,32},{48,40},{56,48},{64,5... | collective-permute-start | bytes 491528 | tf_op jit(solution)/shard_map/ppermute | solution.py:357
  22.1 2.1 %collective-permute-start = (f32[160,128]{1,0:T(8,128)S(1)}, f32[160,128]{1,0:T(8,128)S(1)}, u32[]{:S(2)}, u32[]{:S(2)}) collective-permute-start(f32[160,128]{1,0:T(8,128)S(1)} %get-tuple-element.19.xhi), channel_id=1, source_target_pairs={{0,1},{1,2},{2,3},{3,4},{4,5},{5,6},{6,7},{7,0},{8,9},{9,10},{10,1... | collective-permute-start | bytes 245768 | tf_op jit(solution)/shard_map/ppermute | solution.py:357
  24.1 0.0 collective-permute-start.1
  24.1 13.5 %all_to_all.10.peaks = f32[24,1,128]{2,1,0:T(1,128)S(1)} all-to-all(f32[24,1,128]{2,1,0:T(1,128)S(1)} %get-tuple-element.24), channel_id=1, replica_groups={{704,705,0,1,64,65,128,129,192,193,256,257,320,321,384,385,448,449,512,..., dimensions={0} | all-to-all | bytes 24576 | tf_op jit(solution)/shard_map/all_to_all | solution.py:367
  37.7 1.1 %merge.1 = (f32[32,1,128]{2,1,0:T(1,128)}, f32[128,640]{1,0:T(8,128)S(1)}) custom-call(f32[24,1,128]{2,1,0:T(1,128)S(1)} %all_to_all.10.peaks, f32[5,128,128]{2,1,0:T(8,128)S(1)} %get-tuple-element.17.u, bf16[256,576]{1,0:T(8,128)(2,1)S(1)} %get-tuple-element.25.table), custom_call_target="tpu_custom_call" | custom-call | tf_op jit(solution)/shard_map/merge/pallas_call | solution.py:397
  38.8 0.0 collective-permute-done.xbelow
  38.8 0.0 collective-permute-done.1.xabove
  38.8 0.0 collective-permute-done.2.below
  38.8 0.0 collective-permute-done.3.above
  38.8 0.9 %middle.1 = (f32[5,128,128]{2,1,0:T(8,128)S(1)}, f32[5,128,128]{2,1,0:T(8,128)S(1)}, f32[320,128]{1,0:T(8,128)S(1)}, f32[320,128]{1,0:T(8,128)S(1)}) custom-call(f32[5,128,128]{2,1,0:T(8,128)S(1)} %get-tuple-element.17.u, f32[160,128]{1,0:T(8,128)S(1)} %get-tuple-element.18.xlo, f32[160,128]{1,0:T(8,128)S(1)} %get-tuple-element.19.xhi, ...), custom_call_target="tpu_custom_call" | custom-call | tf_op jit(solution)/shard_map/middle/pallas_call | solution.py:411
  39.8 4.2 %collective-permute-start.4 = (f32[320,128]{1,0:T(8,128)S(1)}, f32[320,128]{1,0:T(8,128)S(1)}, u32[]{:S(2)}, u32[]{:S(2)}) collective-permute-start(f32[320,128]{1,0:T(8,128)S(1)} %get-tuple-element.29), channel_id=1, source_target_pairs={{8,16},{24,32},{40,48},{56,64},{72,80},{88,96},{104,112},{120,128}... | collective-permute-start | bytes 491528 | tf_op jit(solution)/shard_map/ppermute | solution.py:363
  44.0 1.9 %collective-permute-start.5 = (f32[320,128]{1,0:T(8,128)S(1)}, f32[320,128]{1,0:T(8,128)S(1)}, u32[]{:S(2)}, u32[]{:S(2)}) collective-permute-start(f32[320,128]{1,0:T(8,128)S(1)} %get-tuple-element.30), channel_id=1, source_target_pairs={{0,8},{16,24},{32,40},{48,56},{64,72},{80,88},{96,104},{112,120},{... | collective-permute-start | bytes 491528 | tf_op jit(solution)/shard_map/ppermute | solution.py:363
  45.9 8.6 %all-to-all-start.1 = ((f32[32,1,128]{2,1,0:T(1,128)}), f32[32,1,128]{2,1,0:T(1,128)S(1)}, u32[]{:S(2)}, u32[]{:S(2)}) async-start(f32[32,1,128]{2,1,0:T(1,128)} %get-tuple-element.31), calls=%async_computation.1 | async-start | bytes 32768 | tf_op jit(solution)/shard_map/all_to_all | solution.py:367
  55.2 4.9 %all-to-all-done.1.peaks = f32[32,1,128]{2,1,0:T(1,128)S(1)} async-done(((f32[32,1,128]{2,1,0:T(1,128)}), f32[32,1,128]{2,1,0:T(1,128)S(1)}, u32[]{:S(2)}, u32[]{:S(2)}) %all-to-all-start.1) | async-done | bytes 16416 | tf_op jit(solution)/shard_map/all_to_all | solution.py:367
  60.1 0.0 collective-permute-done.4.from_near
  60.1 0.0 collective-permute-done.5.from_far
  60.1 1.4 %last.1 = (f32[5,125,1,128]{3,2,1,0:T(1,128)}, f32[5,25,1,128]{3,2,1,0:T(1,128)}) custom-call(s32[1,1]{1,0:T(1,128)S(6)} %copy.7.shifts, f32[5,128,128]{2,1,0:T(8,128)S(1)} %get-tuple-element.17.u, f32[5,128,128]{2,1,0:T(8,128)S(1)} %get-tuple-element.27.a, f32[5,128,128]{2,1,0:T(8,128)S(1)} %get-tuple-element.28.b, ...), custom_call_target="tpu_custom_call" | custom-call | tf_op jit(solution)/shard_map/last/pallas_call | solution.py:434
Async XLA Ops:
  2.1 36.7 %collective-permute-start.2 = (f32[320,128]{1,0:T(8,128)S(1)}, f32[320,128]{1,0:T(8,128)S(1)}, u32[]{:S(2)}, u32[]{:S(2)}) collective-permute-start(f32[320,128]{1,0:T(8,128)S(1)} %get-tuple-element.20.up), channel_id=1, source_target_pairs={{0,8},{8,16},{16,24},{24,32},{32,40},{40,48},{48,56},{56,64},{64,7... | collective-permute-start | bytes 491528 | tf_op jit(solution)/shard_map/ppermute | solution.py:357
  6.1 32.7 %collective-permute-start.3 = (f32[320,128]{1,0:T(8,128)S(1)}, f32[320,128]{1,0:T(8,128)S(1)}, u32[]{:S(2)}, u32[]{:S(2)}) collective-permute-start(f32[320,128]{1,0:T(8,128)S(1)} %get-tuple-element.21.down), channel_id=1, source_target_pairs={{0,760},{8,0},{16,8},{24,16},{32,24},{40,32},{48,40},{56,48},{64,5... | collective-permute-start | bytes 491528 | tf_op jit(solution)/shard_map/ppermute | solution.py:357
  22.1 16.7 %collective-permute-start = (f32[160,128]{1,0:T(8,128)S(1)}, f32[160,128]{1,0:T(8,128)S(1)}, u32[]{:S(2)}, u32[]{:S(2)}) collective-permute-start(f32[160,128]{1,0:T(8,128)S(1)} %get-tuple-element.19.xhi), channel_id=1, source_target_pairs={{0,1},{1,2},{2,3},{3,4},{4,5},{5,6},{6,7},{7,0},{8,9},{9,10},{10,1... | collective-permute-start | bytes 245768 | tf_op jit(solution)/shard_map/ppermute | solution.py:357
  24.1 14.7 %collective-permute-start.1 = (f32[160,128]{1,0:T(8,128)S(1)}, f32[160,128]{1,0:T(8,128)S(1)}, u32[]{:S(2)}, u32[]{:S(2)}) collective-permute-start(f32[160,128]{1,0:T(8,128)S(1)} %get-tuple-element.18.xlo), channel_id=1, source_target_pairs={{0,7},{1,0},{2,1},{3,2},{4,3},{5,4},{6,5},{7,6},{8,15},{9,8},{10,9... | collective-permute-start | bytes 245768 | tf_op jit(solution)/shard_map/ppermute | solution.py:357
  39.8 20.3 %collective-permute-start.4 = (f32[320,128]{1,0:T(8,128)S(1)}, f32[320,128]{1,0:T(8,128)S(1)}, u32[]{:S(2)}, u32[]{:S(2)}) collective-permute-start(f32[320,128]{1,0:T(8,128)S(1)} %get-tuple-element.29), channel_id=1, source_target_pairs={{8,16},{24,32},{40,48},{56,64},{72,80},{88,96},{104,112},{120,128}... | collective-permute-start | bytes 491528 | tf_op jit(solution)/shard_map/ppermute | solution.py:363
  44.0 16.1 %collective-permute-start.5 = (f32[320,128]{1,0:T(8,128)S(1)}, f32[320,128]{1,0:T(8,128)S(1)}, u32[]{:S(2)}, u32[]{:S(2)}) collective-permute-start(f32[320,128]{1,0:T(8,128)S(1)} %get-tuple-element.30), channel_id=1, source_target_pairs={{0,8},{16,24},{32,40},{48,56},{64,72},{80,88},{96,104},{112,120},{... | collective-permute-start | bytes 491528 | tf_op jit(solution)/shard_map/ppermute | solution.py:363
  45.9 14.1 %all-to-all-start.1 = ((f32[32,1,128]{2,1,0:T(1,128)}), f32[32,1,128]{2,1,0:T(1,128)S(1)}, u32[]{:S(2)}, u32[]{:S(2)}) async-start(f32[32,1,128]{2,1,0:T(1,128)} %get-tuple-element.31), calls=%async_computation.1 | async-start | bytes 32768 | tf_op jit(solution)/shard_map/all_to_all | solution.py:367
